TPU v7x, 32 devices: a whole 2x2x4 slice. The times are simulated.
32 devices in a mesh: groups: 2 (over y), ctx: 4 (over z), chan: 4 (over x, core).
Axes of the slice: x: 2, y: 2, z: 4, core: 2. Of those that a mesh axis runs over, the one named last changes fastest.
Arguments:
- q_feat: bfloat16 [4096, 8192], P(('groups', 'ctx'), 'chan'), parts along dimension 0, may hold values from -6 to 6
- k_feat: bfloat16 [4096, 8192], P(('groups', 'ctx'), 'chan'), parts along dimension 0, may hold values from -6 to 6
- v_feat: bfloat16 [4096, 8192], P(('groups', 'ctx'), 'chan'), parts along dimension 0, may hold values from -6 to 6
- pole_rate: float32 [16, 8192], P(None, 'chan'), may hold values from 4.8828126e-05 to 0.03
- residue: float32 [16, 8192], P(None, 'chan'), may hold values from -1.5 to 1.5
- skip_gain: float32 [8192], P('chan'), may hold values from 0.5 to 1.5
- lengths: int32 [8], P('groups'), parts along dimension 0, may hold values from 1 to 1024, 2048 in all
- owners: int32 [8], P('groups'), parts along dimension 0, may hold values from 0 to 3, as said below
Outputs:
- mixed_out: bfloat16 [4096, 8192], P(('groups', 'ctx'), 'chan'), parts along dimension 0
- decode_state: float32 [8, 16, 8192], P(('groups', 'ctx'), None, 'chan'), parts along dimension 0
There are 2 independent parts, one for each index of `groups`. A program takes and returns all parts, laid end to end along the dimension named above; an argument that names none is the same for every part. Nothing has to cross between parts.
Inputs may be any that keep to these rules, and one draw needn't show every extreme that they name: The 4 lengths sum to 2048; the longest is exactly 1024. The 4 owners are distinct.
All inputs are finite; a program needn't handle non-finite values.
Results may differ from a plain program's by a relative error of at most 0.001.
Values sent between devices are 32-bit elements; how exact they have to be, the bound alone decides.
A program may use at most 128 MiB of HBM per device.

v0:
```python
import jax
import jax.numpy as jnp
from jax import lax
from jax.sharding import PartitionSpec as P

BLOCK = 32


HIGH = lax.Precision.HIGHEST


def from_behind(block, axis, distance):
    devices = range(lax.axis_size(axis))
    route = [(i - distance, i) for i in devices if i - distance in devices]
    return lax.ppermute(block, axis, route)


def shards(q_feat, k_feat, v_feat, pole_rate, residue, skip_gain, lengths, owners):
    tok_dev, channels = q_feat.shape
    pole_count = pole_rate.shape[0]
    request_count = lengths.shape[0]
    ctx_count = lax.axis_size("ctx")
    ctx_index = lax.axis_index("ctx")
    block_len = BLOCK
    block_count = tok_dev // block_len
    first_pos = ctx_index * tok_dev
    dev_last = first_pos + tok_dev - 1
    mixed_in = k_feat.astype(jnp.float32) * v_feat.astype(jnp.float32)
    offsets = jnp.cumsum(lengths) - lengths
    end_pos = offsets + lengths - 1
    positions = first_pos + jnp.arange(tok_dev, dtype=jnp.int32)
    segment = jnp.sum((positions[:, None] >= offsets[None, :]).astype(jnp.int32), axis=1) - 1
    before_seg = jnp.sum((first_pos - 1 >= offsets).astype(jnp.int32)) - 1
    last_seg = segment[tok_dev - 1]
    req_ids = jnp.arange(request_count, dtype=jnp.int32)
    scaled_res = residue * jnp.sqrt(1.0 - jnp.exp(-2.0 * pole_rate))
    step_float = jnp.arange(block_len, dtype=jnp.float32)
    decay_table = jnp.exp(-pole_rate[:, None, :] * step_float[None, :, None])
    decay_next = jnp.exp(-pole_rate[:, None, :] * (step_float[None, :, None] + 1.0))
    decay_back = decay_table[:, ::-1, :]
    block_decay = jnp.exp(-pole_rate * block_len)
    kernel = jnp.sum(scaled_res[:, None, :] * decay_table, axis=0)
    lag_steps = jnp.arange(block_len)[:, None] - jnp.arange(block_len)[None, :]
    toeplitz = jnp.where(
        (lag_steps >= 0)[:, :, None], kernel[jnp.clip(lag_steps, 0, block_len - 1)], 0.0
    )
    ref_pos = jnp.minimum(end_pos, dev_last)

    def block_step(loop_carry, block_inputs):
        mode_state, carry_seg, request_acc = loop_carry
        u_block, seg_block, block_index = block_inputs
        same_seg = (seg_block[:, None] == seg_block[None, :]).astype(jnp.float32)
        intra = jnp.einsum("ts,tsc,sc->tc", same_seg, toeplitz, u_block, precision=HIGH)
        live_mask = (seg_block == carry_seg).astype(jnp.float32)
        carried = (
            jnp.einsum("ptc,pc->tc", decay_next, scaled_res * mode_state, precision=HIGH)
            * live_mask[:, None]
        )
        seg_end = seg_block[block_len - 1]
        keep_mask = (carry_seg == seg_end).astype(jnp.float32)
        weighted = u_block * (seg_block == seg_end).astype(jnp.float32)[:, None]
        new_state = block_decay * mode_state * keep_mask + jnp.einsum(
            "psc,sc->pc", decay_back, weighted, precision=HIGH
        )
        block_end = first_pos + block_index * block_len + block_len - 1
        member = (seg_block[None, :] == req_ids[:, None]).astype(jnp.float32)
        collected = jnp.einsum("rs,psc,sc->rpc", member, decay_back, u_block, precision=HIGH)
        offset_steps = jnp.maximum(ref_pos - block_end, -(block_len - 1)).astype(jnp.float32)
        request_acc = (
            request_acc + jnp.exp(-pole_rate[None, :, :] * offset_steps[:, None, None]) * collected
        )
        return ((new_state, seg_end, request_acc), intra + carried)

    init_carry = (
        jnp.zeros((pole_count, channels), jnp.float32),
        before_seg,
        jnp.zeros((request_count, pole_count, channels), jnp.float32),
    )
    block_inputs = (
        mixed_in.reshape(block_count, block_len, channels),
        segment.reshape(block_count, block_len),
        jnp.arange(block_count, dtype=jnp.int32),
    )
    (local_end, seg_final, request_acc), local_out = lax.scan(block_step, init_carry, block_inputs)
    pass_mask = (last_seg == before_seg).astype(jnp.float32)
    span_decay = jnp.exp(-pole_rate * tok_dev) * pass_mask

    def relay_step(turn_index, incoming_now):
        outgoing = span_decay * incoming_now + local_end
        return from_behind(outgoing, "ctx", 1)

    incoming = lax.fori_loop(0, ctx_count - 1, relay_step, jnp.zeros_like(local_end))
    start_decay = jnp.exp(
        -pole_rate[None, :, :]
        * (jnp.arange(block_count, dtype=jnp.float32) * block_len)[:, None, None]
    )
    correction = jnp.einsum(
        "kpc,ptc->ktc",
        start_decay * (scaled_res * incoming)[None, :, :],
        decay_next,
        precision=HIGH,
    )
    live_dev = (segment == before_seg).astype(jnp.float32)
    conv = (
        local_out.reshape(tok_dev, channels)
        + correction.reshape(tok_dev, channels) * live_dev[:, None]
    )
    mixed_out = (q_feat.astype(jnp.float32) * (conv + skip_gain[None, :] * mixed_in)).astype(
        jnp.bfloat16
    )
    slot_ids = jnp.arange(ctx_count, dtype=jnp.int32)
    placement = (owners[None, :] == slot_ids[:, None]).astype(jnp.float32)
    ends_here = ((end_pos >= first_pos) & (end_pos <= dev_last)).astype(jnp.float32)
    from_before = (req_ids == before_seg).astype(jnp.float32)
    reach_steps = jnp.maximum(end_pos - first_pos + 1, 0).astype(jnp.float32)
    carried_in = jnp.exp(-pole_rate[None, :, :] * reach_steps[:, None, None]) * incoming[None, :, :]
    finished = (request_acc + from_before[:, None, None] * carried_in) * ends_here[:, None, None]
    slotted = jnp.einsum("qr,rpc->qpc", placement, finished, precision=HIGH)
    slotted = slotted.reshape(ctx_count, 1, pole_count, channels)
    received = lax.all_to_all(slotted, "ctx", split_axis=0, concat_axis=0, tiled=True)
    decode_state = jnp.sum(received, axis=0)
    return (mixed_out, decode_state)


def solution(mesh):
    placed = (
        P(("groups", "ctx"), "chan"),
        P(("groups", "ctx"), "chan"),
        P(("groups", "ctx"), "chan"),
        P(None, "chan"),
        P(None, "chan"),
        P("chan"),
        P("groups"),
        P("groups"),
    )
    return jax.shard_map(
        shards,
        mesh=mesh,
        in_specs=placed,
        out_specs=(P(("groups", "ctx"), "chan"), P(("groups", "ctx"), None, "chan")),
        check_vma=False,
    )
```

profile of v0, /device:TPU:0, one launch (start us, length us, event | category | flops | bytes accessed | tf_op | source)
XLA Modules:
  0.0 428.8 jit_solution(18111155510862013643)
XLA Ops:
  7.8 4.4 %multiply_reduce_fusion.2 = (f32[32,2048]{1,0:T(8,128)S(1)}, f32[16,32,2048]{2,1,0:T(8,128)}, f32[16,32,2048]{2,1,0:T(8,128)}) fusion(f32[16,2048]{1,0:T(8,128)S(1)} %get-tuple-element.641, f32[16,2048]{1,0:T(8,128)S(1)} %get-tuple-element.643, f32[32]{0:T(128)S(1)} %iota_add_fusion.1), kind=kLoop, calls=%fused_computation.47 | loop fusion | flops 4128768 | bytes 8913024 | tf_op jit(solution)/shard_map/reduce_sum | solution.py:42
  12.2 10.5 %rev.3 = f32[16,32,2048]{2,1,0:T(8,128)} reverse(f32[16,32,2048]{2,1,0:T(8,128)} %get-tuple-element.475), dimensions={1} | reverse | bytes 8388608 | tf_op jit(solution)/shard_map/rev | solution.py:40
  22.7 4.3 %convert_multiply_fusion = f32[512,2048]{1,0:T(8,128)} fusion(bf16[512,2048]{1,0:T(8,128)(2,1)S(1)} %copy-done.1, bf16[512,2048]{1,0:T(8,128)(2,1)} %param.13), kind=kLoop, calls=%fused_computation.49 | loop fusion | flops 3145728 | bytes 8388608 | tf_op jit(solution)/shard_map/mul | solution.py:28
  27.0 6.9 %gather_fusion = f32[1024,2048]{1,0:T(8,128)} fusion(f32[32,2048]{1,0:T(8,128)S(1)} %get-tuple-element.473, s32[1024]{0:T(1024)S(1)} %broadcast_clamp_fusion), kind=kCustom, calls=%fused_computation | custom fusion | bytes 16781312 | tf_op jit(solution)/shard_map/gather | solution.py:45
  33.9 7.3 %broadcast_select_fusion = f32[32,32,2048]{2,1,0:T(8,128)} fusion(f32[32,32,2048]{2,1,0:T(8,128)} %bitcast.125, pred[32,32]{1,0:T(8,128)(4,1)S(1)} %subtract_compare_fusion), kind=kLoop, calls=%fused_computation.46 | loop fusion | flops 2097152 | bytes 16778240 | tf_op jit(solution)/shard_map/jit(_where)/select_n | solution.py:44
  41.2 297.4 %while.32 = (s32[]{:T(128)}, f32[16,2048]{1,0:T(8,128)S(1)}, s32[]{:T(128)}, f32[4,16,2048]{2,0,1:T(4,128)S(1)}, f32[16,32,2048]{2,1,0:T(8,128)}, /*index=5*/f32...) while((s32[]{:T(128)}, f32[16,2048]{1,0:T(8,128)S(1)}, ...), condition=%wide.region_5.6_spmd.clone, body=%wide.region_4.5_spmd.clone.sunk | while | flops 84673808 | bytes 38801028 | solution.py:84
  45.8 2.9 multiply_reduce_fusion.5
  48.8 6.9 %fusion.66 = f32[32,1,2048]{2,1,0:T(1,128)S(1)} fusion(f32[32,32,2048]{2,1,0:T(8,128)} %get-tuple-element.682, f32[32,2048]{1,0:T(8,128)S(1)} %get-tuple-element.624, pred[32,32,1]{1,0,2:T(32,128)(4,1)S(1)} %compare_bitcast_fusion.2), kind=kOutput, calls=%fused_computation.4.clone.1 | convolution fusion | flops 27262976 | bytes 8913920 | tf_op jit(solution)/shard_map/while/body/eval_jaxpr/ts,tsc,sc->tc/dot_general | solution.py:53
  67.3 6.9 %fusion.66 = f32[32,1,2048]{2,1,0:T(1,128)S(1)} fusion(f32[32,32,2048]{2,1,0:T(8,128)} %get-tuple-element.682, f32[32,2048]{1,0:T(8,128)S(1)} %get-tuple-element.624, pred[32,32,1]{1,0,2:T(32,128)(4,1)S(1)} %compare_bitcast_fusion.2), kind=kOutput, calls=%fused_computation.4.clone.1 | convolution fusion | flops 27262976 | bytes 8913920 | tf_op jit(solution)/shard_map/while/body/eval_jaxpr/ts,tsc,sc->tc/dot_general | solution.py:53
  85.9 6.9 %fusion.66 = f32[32,1,2048]{2,1,0:T(1,128)S(1)} fusion(f32[32,32,2048]{2,1,0:T(8,128)} %get-tuple-element.682, f32[32,2048]{1,0:T(8,128)S(1)} %get-tuple-element.624, pred[32,32,1]{1,0,2:T(32,128)(4,1)S(1)} %compare_bitcast_fusion.2), kind=kOutput, calls=%fused_computation.4.clone.1 | convolution fusion | flops 27262976 | bytes 8913920 | tf_op jit(solution)/shard_map/while/body/eval_jaxpr/ts,tsc,sc->tc/dot_general | solution.py:53
  104.5 6.9 %fusion.66 = f32[32,1,2048]{2,1,0:T(1,128)S(1)} fusion(f32[32,32,2048]{2,1,0:T(8,128)} %get-tuple-element.682, f32[32,2048]{1,0:T(8,128)S(1)} %get-tuple-element.624, pred[32,32,1]{1,0,2:T(32,128)(4,1)S(1)} %compare_bitcast_fusion.2), kind=kOutput, calls=%fused_computation.4.clone.1 | convolution fusion | flops 27262976 | bytes 8913920 | tf_op jit(solution)/shard_map/while/body/eval_jaxpr/ts,tsc,sc->tc/dot_general | solution.py:53
  123.1 6.9 %fusion.66 = f32[32,1,2048]{2,1,0:T(1,128)S(1)} fusion(f32[32,32,2048]{2,1,0:T(8,128)} %get-tuple-element.682, f32[32,2048]{1,0:T(8,128)S(1)} %get-tuple-element.624, pred[32,32,1]{1,0,2:T(32,128)(4,1)S(1)} %compare_bitcast_fusion.2), kind=kOutput, calls=%fused_computation.4.clone.1 | convolution fusion | flops 27262976 | bytes 8913920 | tf_op jit(solution)/shard_map/while/body/eval_jaxpr/ts,tsc,sc->tc/dot_general | solution.py:53
  141.7 6.9 %fusion.66 = f32[32,1,2048]{2,1,0:T(1,128)S(1)} fusion(f32[32,32,2048]{2,1,0:T(8,128)} %get-tuple-element.682, f32[32,2048]{1,0:T(8,128)S(1)} %get-tuple-element.624, pred[32,32,1]{1,0,2:T(32,128)(4,1)S(1)} %compare_bitcast_fusion.2), kind=kOutput, calls=%fused_computation.4.clone.1 | convolution fusion | flops 27262976 | bytes 8913920 | tf_op jit(solution)/shard_map/while/body/eval_jaxpr/ts,tsc,sc->tc/dot_general | solution.py:53
  160.3 6.9 %fusion.66 = f32[32,1,2048]{2,1,0:T(1,128)S(1)} fusion(f32[32,32,2048]{2,1,0:T(8,128)} %get-tuple-element.682, f32[32,2048]{1,0:T(8,128)S(1)} %get-tuple-element.624, pred[32,32,1]{1,0,2:T(32,128)(4,1)S(1)} %compare_bitcast_fusion.2), kind=kOutput, calls=%fused_computation.4.clone.1 | convolution fusion | flops 27262976 | bytes 8913920 | tf_op jit(solution)/shard_map/while/body/eval_jaxpr/ts,tsc,sc->tc/dot_general | solution.py:53
  178.9 6.9 %fusion.66 = f32[32,1,2048]{2,1,0:T(1,128)S(1)} fusion(f32[32,32,2048]{2,1,0:T(8,128)} %get-tuple-element.682, f32[32,2048]{1,0:T(8,128)S(1)} %get-tuple-element.624, pred[32,32,1]{1,0,2:T(32,128)(4,1)S(1)} %compare_bitcast_fusion.2), kind=kOutput, calls=%fused_computation.4.clone.1 | convolution fusion | flops 27262976 | bytes 8913920 | tf_op jit(solution)/shard_map/while/body/eval_jaxpr/ts,tsc,sc->tc/dot_general | solution.py:53
  197.4 6.9 %fusion.66 = f32[32,1,2048]{2,1,0:T(1,128)S(1)} fusion(f32[32,32,2048]{2,1,0:T(8,128)} %get-tuple-element.682, f32[32,2048]{1,0:T(8,128)S(1)} %get-tuple-element.624, pred[32,32,1]{1,0,2:T(32,128)(4,1)S(1)} %compare_bitcast_fusion.2), kind=kOutput, calls=%fused_computation.4.clone.1 | convolution fusion | flops 27262976 | bytes 8913920 | tf_op jit(solution)/shard_map/while/body/eval_jaxpr/ts,tsc,sc->tc/dot_general | solution.py:53
  216.0 6.9 %fusion.66 = f32[32,1,2048]{2,1,0:T(1,128)S(1)} fusion(f32[32,32,2048]{2,1,0:T(8,128)} %get-tuple-element.682, f32[32,2048]{1,0:T(8,128)S(1)} %get-tuple-element.624, pred[32,32,1]{1,0,2:T(32,128)(4,1)S(1)} %compare_bitcast_fusion.2), kind=kOutput, calls=%fused_computation.4.clone.1 | convolution fusion | flops 27262976 | bytes 8913920 | tf_op jit(solution)/shard_map/while/body/eval_jaxpr/ts,tsc,sc->tc/dot_general | solution.py:53
  234.6 6.9 %fusion.66 = f32[32,1,2048]{2,1,0:T(1,128)S(1)} fusion(f32[32,32,2048]{2,1,0:T(8,128)} %get-tuple-element.682, f32[32,2048]{1,0:T(8,128)S(1)} %get-tuple-element.624, pred[32,32,1]{1,0,2:T(32,128)(4,1)S(1)} %compare_bitcast_fusion.2), kind=kOutput, calls=%fused_computation.4.clone.1 | convolution fusion | flops 27262976 | bytes 8913920 | tf_op jit(solution)/shard_map/while/body/eval_jaxpr/ts,tsc,sc->tc/dot_general | solution.py:53
  253.2 6.9 %fusion.66 = f32[32,1,2048]{2,1,0:T(1,128)S(1)} fusion(f32[32,32,2048]{2,1,0:T(8,128)} %get-tuple-element.682, f32[32,2048]{1,0:T(8,128)S(1)} %get-tuple-element.624, pred[32,32,1]{1,0,2:T(32,128)(4,1)S(1)} %compare_bitcast_fusion.2), kind=kOutput, calls=%fused_computation.4.clone.1 | convolution fusion | flops 27262976 | bytes 8913920 | tf_op jit(solution)/shard_map/while/body/eval_jaxpr/ts,tsc,sc->tc/dot_general | solution.py:53
  271.8 6.9 %fusion.66 = f32[32,1,2048]{2,1,0:T(1,128)S(1)} fusion(f32[32,32,2048]{2,1,0:T(8,128)} %get-tuple-element.682, f32[32,2048]{1,0:T(8,128)S(1)} %get-tuple-element.624, pred[32,32,1]{1,0,2:T(32,128)(4,1)S(1)} %compare_bitcast_fusion.2), kind=kOutput, calls=%fused_computation.4.clone.1 | convolution fusion | flops 27262976 | bytes 8913920 | tf_op jit(solution)/shard_map/while/body/eval_jaxpr/ts,tsc,sc->tc/dot_general | solution.py:53
  290.4 6.9 %fusion.66 = f32[32,1,2048]{2,1,0:T(1,128)S(1)} fusion(f32[32,32,2048]{2,1,0:T(8,128)} %get-tuple-element.682, f32[32,2048]{1,0:T(8,128)S(1)} %get-tuple-element.624, pred[32,32,1]{1,0,2:T(32,128)(4,1)S(1)} %compare_bitcast_fusion.2), kind=kOutput, calls=%fused_computation.4.clone.1 | convolution fusion | flops 27262976 | bytes 8913920 | tf_op jit(solution)/shard_map/while/body/eval_jaxpr/ts,tsc,sc->tc/dot_general | solution.py:53
  309.0 6.9 %fusion.66 = f32[32,1,2048]{2,1,0:T(1,128)S(1)} fusion(f32[32,32,2048]{2,1,0:T(8,128)} %get-tuple-element.682, f32[32,2048]{1,0:T(8,128)S(1)} %get-tuple-element.624, pred[32,32,1]{1,0,2:T(32,128)(4,1)S(1)} %compare_bitcast_fusion.2), kind=kOutput, calls=%fused_computation.4.clone.1 | convolution fusion | flops 27262976 | bytes 8913920 | tf_op jit(solution)/shard_map/while/body/eval_jaxpr/ts,tsc,sc->tc/dot_general | solution.py:53
  327.5 6.9 %fusion.66 = f32[32,1,2048]{2,1,0:T(1,128)S(1)} fusion(f32[32,32,2048]{2,1,0:T(8,128)} %get-tuple-element.682, f32[32,2048]{1,0:T(8,128)S(1)} %get-tuple-element.624, pred[32,32,1]{1,0,2:T(32,128)(4,1)S(1)} %compare_bitcast_fusion.2), kind=kOutput, calls=%fused_computation.4.clone.1 | convolution fusion | flops 27262976 | bytes 8913920 | tf_op jit(solution)/shard_map/while/body/eval_jaxpr/ts,tsc,sc->tc/dot_general | solution.py:53
  338.6 21.6 %while.31 = (s32[]{:T(128)}, f32[16,2048]{1,0:T(8,128)S(1)}, f32[16,2048]{1,0:T(8,128)S(1)}, f32[16,2048]{1,0:T(8,128)S(1)}, s32[]{:T(128)}) while((s32[]{:T(128)}, f32[16,2048]{1,0:T(8,128)S(1)}, f32[16,2048]{1,0:T(8,128)S(1)}, f32[16,2048]{1,0:T(8,128)S(1)}, s32[]{:T(128)}) %tuple.78), condition=%wide.region_7.8_spmd, body=%wide.region_6.7_spmd.sunk | while | flops 65538 | bytes 1048677 | solution.py:92
  338.6 5.0 %collective-permute-start = (f32[16,2048]{1,0:T(8,128)S(1)}, f32[16,2048]{1,0:T(8,128)S(1)}, u32[]{:S(2)}, u32[]{:S(2)}) collective-permute-start(f32[16,2048]{1,0:T(8,128)S(1)} %multiply_add_fusion.2), channel_id=1, source_target_pairs={{0,4},{4,8},{8,12},{1,5},{5,9},{9,13},{2,6},{6,10},{10,14},{3,7},{... | collective-permute-start | bytes 393224 | tf_op jit(solution)/shard_map/while/body/eval_jaxpr/ppermute | solution.py:15
  346.3 4.4 %collective-permute-start = (f32[16,2048]{1,0:T(8,128)S(1)}, f32[16,2048]{1,0:T(8,128)S(1)}, u32[]{:S(2)}, u32[]{:S(2)}) collective-permute-start(f32[16,2048]{1,0:T(8,128)S(1)} %multiply_add_fusion.2), channel_id=1, source_target_pairs={{0,4},{4,8},{8,12},{1,5},{5,9},{9,13},{2,6},{6,10},{10,14},{3,7},{... | collective-permute-start | bytes 393224 | tf_op jit(solution)/shard_map/while/body/eval_jaxpr/ppermute | solution.py:15
  353.2 4.4 %collective-permute-start = (f32[16,2048]{1,0:T(8,128)S(1)}, f32[16,2048]{1,0:T(8,128)S(1)}, u32[]{:S(2)}, u32[]{:S(2)}) collective-permute-start(f32[16,2048]{1,0:T(8,128)S(1)} %multiply_add_fusion.2), channel_id=1, source_target_pairs={{0,4},{4,8},{8,12},{1,5},{5,9},{9,13},{2,6},{6,10},{10,14},{3,7},{... | collective-permute-start | bytes 393224 | tf_op jit(solution)/shard_map/while/body/eval_jaxpr/ppermute | solution.py:15
  363.1 5.7 %all-to-all-start = ((f32[4,1,16,2048]{3,2,1,0:T(8,128)}), f32[4,1,16,2048]{3,2,1,0:T(8,128)}, u32[]{:S(2)}, u32[]{:S(2)}) async-start(f32[4,1,16,2048]{3,2,1,0:T(8,128)} %copy.27), calls=%async_computation | async-start | bytes 1048576 | tf_op jit(solution)/shard_map/all_to_all | solution.py:120
  371.5 12.6 %copy.25 = f32[16,32,2048]{1,0,2:T(8,128)} copy(f32[16,32,2048]{2,1,0:T(8,128)} %get-tuple-element.474) | data formatting | bytes 8388608 | tf_op jit(solution)/shard_map/exp | solution.py:39
  384.1 23.6 %fusion.29 = f32[16,32,2048]{1,0,2:T(8,128)} fusion(f32[16,32,2048]{1,0,2:T(8,128)} %copy.25, f32[16,2048]{0,1:T(8,128)} %copy.24, f32[16]{0:T(128)S(1)} %iota_multiply_fusion, f32[16,2048]{0,1:T(8,128)S(1)} %copy-done.2), kind=kOutput, calls=%fused_computation.36 | convolution fusion | flops 202375168 | bytes 8650816 | tf_op jit(solution)/shard_map/kpc,ptc->ktc/dot_general | solution.py:97
  407.7 11.5 %copy.26 = f32[16,32,2048]{2,1,0:T(8,128)} copy(f32[16,32,2048]{1,0,2:T(8,128)} %fusion.29) | data formatting | bytes 8388608 | tf_op jit(solution)/shard_map/kpc,ptc->ktc/transpose | solution.py:97
  419.2 7.8 %fusion.38 = bf16[512,2048]{1,0:T(8,128)(2,1)} fusion(f32[16,32,2048]{2,1,0:T(8,128)} %copy.26, f32[16,32,2048]{2,1,0:T(8,128)} %get-tuple-element.359, bf16[512,2048]{1,0:T(8,128)(2,1)} %param.12, f32[2048]{0:T(1024)S(1)} %copy-done.6, f32[512]{0:T(512)S(1)} %compare_convert_fusion.3, bf16[512,2048]{1,0:T(8,128)(2,1)S(1)} %copy-done.1, ...), kind=kLoop, calls=%fused_computation.44 | loop fusion | flops 10485760 | bytes 16787456 | tf_op jit(solution)/shard_map/convert_element_type | solution.py:108
  (273 shorter events, 178.0 us)
Async XLA Ops:
  7.8 4.5 %copy-start.3 = (f32[16,2048]{1,0:T(8,128)}, f32[16,2048]{1,0:T(8,128)S(1)}, u32[]{:S(2)}) copy-start(f32[16,2048]{1,0:T(8,128)S(1)} %get-tuple-element.643) | copy-start | bytes 393220
  12.2 10.5 %copy-start.1 = (bf16[512,2048]{1,0:T(8,128)(2,1)S(1)}, bf16[512,2048]{1,0:T(8,128)(2,1)}, u32[]{:S(2)}) copy-start(bf16[512,2048]{1,0:T(8,128)(2,1)} %param.14) | copy-start | bytes 6291460
  33.9 7.3 %copy-start.4 = (f32[16,2048]{1,0:T(8,128)S(1)}, f32[16,2048]{1,0:T(8,128)}, u32[]{:S(2)}) copy-start(f32[16,2048]{1,0:T(8,128)} %copy-done.3) | copy-start | bytes 393220
  33.9 7.3 %copy-start.8 = (s32[4]{0:T(128)S(1)}, s32[4]{0:T(128)}, u32[]{:S(2)}) copy-start(s32[4]{0:T(128)} %get-tuple-element.639) | copy-start | bytes 52
  41.1 319.0 %copy-start.7 = (f32[4]{0:T(128)S(1)}, f32[4]{0:T(128)}, u32[]{:S(2)}) copy-start(f32[4]{0:T(128)} %get-tuple-element.481) | copy-start | bytes 52
  48.7 6.9 %copy-start = (f32[16,32,2048]{2,1,0:T(8,128)S(1)}, f32[16,32,2048]{2,1,0:T(8,128)}, u32[]{:S(2)}) copy-start(f32[16,32,2048]{2,1,0:T(8,128)} %get-tuple-element.677) | copy-start | bytes 12582916 | tf_op jit(solution)/shard_map/while
  67.3 6.9 %copy-start = (f32[16,32,2048]{2,1,0:T(8,128)S(1)}, f32[16,32,2048]{2,1,0:T(8,128)}, u32[]{:S(2)}) copy-start(f32[16,32,2048]{2,1,0:T(8,128)} %get-tuple-element.677) | copy-start | bytes 12582916 | tf_op jit(solution)/shard_map/while
  85.9 6.9 %copy-start = (f32[16,32,2048]{2,1,0:T(8,128)S(1)}, f32[16,32,2048]{2,1,0:T(8,128)}, u32[]{:S(2)}) copy-start(f32[16,32,2048]{2,1,0:T(8,128)} %get-tuple-element.677) | copy-start | bytes 12582916 | tf_op jit(solution)/shard_map/while
  104.5 6.9 %copy-start = (f32[16,32,2048]{2,1,0:T(8,128)S(1)}, f32[16,32,2048]{2,1,0:T(8,128)}, u32[]{:S(2)}) copy-start(f32[16,32,2048]{2,1,0:T(8,128)} %get-tuple-element.677) | copy-start | bytes 12582916 | tf_op jit(solution)/shard_map/while
  123.1 6.9 %copy-start = (f32[16,32,2048]{2,1,0:T(8,128)S(1)}, f32[16,32,2048]{2,1,0:T(8,128)}, u32[]{:S(2)}) copy-start(f32[16,32,2048]{2,1,0:T(8,128)} %get-tuple-element.677) | copy-start | bytes 12582916 | tf_op jit(solution)/shard_map/while
  141.7 6.9 %copy-start = (f32[16,32,2048]{2,1,0:T(8,128)S(1)}, f32[16,32,2048]{2,1,0:T(8,128)}, u32[]{:S(2)}) copy-start(f32[16,32,2048]{2,1,0:T(8,128)} %get-tuple-element.677) | copy-start | bytes 12582916 | tf_op jit(solution)/shard_map/while
  160.3 6.9 %copy-start = (f32[16,32,2048]{2,1,0:T(8,128)S(1)}, f32[16,32,2048]{2,1,0:T(8,128)}, u32[]{:S(2)}) copy-start(f32[16,32,2048]{2,1,0:T(8,128)} %get-tuple-element.677) | copy-start | bytes 12582916 | tf_op jit(solution)/shard_map/while
  178.8 6.9 %copy-start = (f32[16,32,2048]{2,1,0:T(8,128)S(1)}, f32[16,32,2048]{2,1,0:T(8,128)}, u32[]{:S(2)}) copy-start(f32[16,32,2048]{2,1,0:T(8,128)} %get-tuple-element.677) | copy-start | bytes 12582916 | tf_op jit(solution)/shard_map/while
  197.4 6.9 %copy-start = (f32[16,32,2048]{2,1,0:T(8,128)S(1)}, f32[16,32,2048]{2,1,0:T(8,128)}, u32[]{:S(2)}) copy-start(f32[16,32,2048]{2,1,0:T(8,128)} %get-tuple-element.677) | copy-start | bytes 12582916 | tf_op jit(solution)/shard_map/while
  216.0 6.9 %copy-start = (f32[16,32,2048]{2,1,0:T(8,128)S(1)}, f32[16,32,2048]{2,1,0:T(8,128)}, u32[]{:S(2)}) copy-start(f32[16,32,2048]{2,1,0:T(8,128)} %get-tuple-element.677) | copy-start | bytes 12582916 | tf_op jit(solution)/shard_map/while
  234.6 6.9 %copy-start = (f32[16,32,2048]{2,1,0:T(8,128)S(1)}, f32[16,32,2048]{2,1,0:T(8,128)}, u32[]{:S(2)}) copy-start(f32[16,32,2048]{2,1,0:T(8,128)} %get-tuple-element.677) | copy-start | bytes 12582916 | tf_op jit(solution)/shard_map/while
  253.2 6.9 %copy-start = (f32[16,32,2048]{2,1,0:T(8,128)S(1)}, f32[16,32,2048]{2,1,0:T(8,128)}, u32[]{:S(2)}) copy-start(f32[16,32,2048]{2,1,0:T(8,128)} %get-tuple-element.677) | copy-start | bytes 12582916 | tf_op jit(solution)/shard_map/while
  271.8 6.9 %copy-start = (f32[16,32,2048]{2,1,0:T(8,128)S(1)}, f32[16,32,2048]{2,1,0:T(8,128)}, u32[]{:S(2)}) copy-start(f32[16,32,2048]{2,1,0:T(8,128)} %get-tuple-element.677) | copy-start | bytes 12582916 | tf_op jit(solution)/shard_map/while
  290.4 6.9 %copy-start = (f32[16,32,2048]{2,1,0:T(8,128)S(1)}, f32[16,32,2048]{2,1,0:T(8,128)}, u32[]{:S(2)}) copy-start(f32[16,32,2048]{2,1,0:T(8,128)} %get-tuple-element.677) | copy-start | bytes 12582916 | tf_op jit(solution)/shard_map/while
  308.9 6.9 %copy-start = (f32[16,32,2048]{2,1,0:T(8,128)S(1)}, f32[16,32,2048]{2,1,0:T(8,128)}, u32[]{:S(2)}) copy-start(f32[16,32,2048]{2,1,0:T(8,128)} %get-tuple-element.677) | copy-start | bytes 12582916 | tf_op jit(solution)/shard_map/while
  327.5 6.9 %copy-start = (f32[16,32,2048]{2,1,0:T(8,128)S(1)}, f32[16,32,2048]{2,1,0:T(8,128)}, u32[]{:S(2)}) copy-start(f32[16,32,2048]{2,1,0:T(8,128)} %get-tuple-element.677) | copy-start | bytes 12582916 | tf_op jit(solution)/shard_map/while
  338.5 30.3 %copy-start.5 = (f32[16,2048]{1,0:T(8,128)S(1)}, f32[16,2048]{1,0:T(8,128)}, u32[]{:S(2)}) copy-start(f32[16,2048]{1,0:T(8,128)} %copy-done.3) | copy-start | bytes 393220
  338.6 7.7 %collective-permute-start = (f32[16,2048]{1,0:T(8,128)S(1)}, f32[16,2048]{1,0:T(8,128)S(1)}, u32[]{:S(2)}, u32[]{:S(2)}) collective-permute-start(f32[16,2048]{1,0:T(8,128)S(1)} %multiply_add_fusion.2), channel_id=1, source_target_pairs={{0,4},{4,8},{8,12},{1,5},{5,9},{9,13},{2,6},{6,10},{10,14},{3,7},{... | collective-permute-start | bytes 393224 | tf_op jit(solution)/shard_map/while/body/eval_jaxpr/ppermute | solution.py:15
  346.3 6.9 %collective-permute-start = (f32[16,2048]{1,0:T(8,128)S(1)}, f32[16,2048]{1,0:T(8,128)S(1)}, u32[]{:S(2)}, u32[]{:S(2)}) collective-permute-start(f32[16,2048]{1,0:T(8,128)S(1)} %multiply_add_fusion.2), channel_id=1, source_target_pairs={{0,4},{4,8},{8,12},{1,5},{5,9},{9,13},{2,6},{6,10},{10,14},{3,7},{... | collective-permute-start | bytes 393224 | tf_op jit(solution)/shard_map/while/body/eval_jaxpr/ppermute | solution.py:15
  353.2 6.9 %collective-permute-start = (f32[16,2048]{1,0:T(8,128)S(1)}, f32[16,2048]{1,0:T(8,128)S(1)}, u32[]{:S(2)}, u32[]{:S(2)}) collective-permute-start(f32[16,2048]{1,0:T(8,128)S(1)} %multiply_add_fusion.2), channel_id=1, source_target_pairs={{0,4},{4,8},{8,12},{1,5},{5,9},{9,13},{2,6},{6,10},{10,14},{3,7},{... | collective-permute-start | bytes 393224 | tf_op jit(solution)/shard_map/while/body/eval_jaxpr/ppermute | solution.py:15
  363.1 64.0 %all-to-all-start = ((f32[4,1,16,2048]{3,2,1,0:T(8,128)}), f32[4,1,16,2048]{3,2,1,0:T(8,128)}, u32[]{:S(2)}, u32[]{:S(2)}) async-start(f32[4,1,16,2048]{3,2,1,0:T(8,128)} %copy.27), calls=%async_computation | async-start | bytes 1048576 | tf_op jit(solution)/shard_map/all_to_all | solution.py:120
  371.5 12.6 %copy-start.2 = (f32[16,2048]{0,1:T(8,128)S(1)}, f32[16,2048]{0,1:T(8,128)}, u32[]{:S(2)}) copy-start(f32[16,2048]{0,1:T(8,128)} %copy.23) | copy-start | bytes 393220
  407.7 11.5 %copy-start.6 = (f32[2048]{0:T(1024)S(1)}, f32[2048]{0:T(1024)}, u32[]{:S(2)}) copy-start(f32[2048]{0:T(1024)} %param.17) | copy-start | bytes 24580
where the time goes:
time: 432 us; the launch traced here: 429 us
  matrix products  167 us (39%)
  other arithmetic  141 us (33%)
  local copies, waits for them, and re-layouts  64.3 us (15%)
  loops' own time  27.7 us (6%)
  starting transfers between devices  19.5 us (5%)
  waiting for transfers between devices  7.71 us (2%)
    dot_general x16, matrix products, block_step(): jnp.einsum('ts,tsc,sc->tc', same_seg, toeplitz, u_block, precision=HIGH)  110 us
    dot_general x16, other arithmetic, block_step(): jnp.einsum('psc,sc->pc', decay_back, weighted, precision=HIGH)  46.1 us
    dot_general x16, matrix products, block_step(): jnp.einsum('rs,psc,sc->rpc', member, decay_back, u_block, precision=HIGH)  31.5 us
    another operation x1, loops' own time, shards(): lax.scan(block_step, init_carry, block_inputs)  27.6 us
    dot_general x1, matrix products, shards(): jnp.einsum('kpc,ptc->ktc', start_decay * (scaled_res * incoming)[None, :,...  23.6 us
    while x32, other arithmetic  18 us
    ppermute x3, starting transfers between devices, from_behind(): return lax.ppermute(block, axis, route)  13.7 us
    dynamic_update_slice x16, other arithmetic, shards(): lax.scan(block_step, init_carry, block_inputs)  13.3 us
  transfers between devices with their start and end apart: 4, of which 3 were waited for; matrix products, arithmetic and copies ran while one was open for 14% of the time, Pallas kernels for 0%

commit v1 on v0

v1 whole, which is shorter than its diff:
```python
import functools

import jax
import jax.numpy as jnp
from jax import lax
from jax.experimental import pallas as pl
from jax.experimental.pallas import tpu as pltpu
from jax.sharding import PartitionSpec as P

F32 = jnp.float32
LANES = 128
ROWS = 8
UNROLL = 8


def spans(lens_ref, count, tok):
    first = lax.axis_index("ctx") * tok
    offset = jnp.int32(0)
    found = []
    for r in range(count):
        size = lens_ref[r]
        end = offset + size
        lo = jnp.clip(offset - first, 0, tok)
        hi = jnp.clip(end - first, 0, tok)
        found.append((lo, hi, offset < first, end > first, end <= first + tok, end - first))
        offset = end
    return found


def spread(value, dst_ref, sub, base=0):
    for i in range(value.shape[0] // ROWS):
        for j in range(sub):
            dst_ref[pl.ds(base + i * ROWS * sub + j, ROWS, stride=sub), :] = value[
                i * ROWS : (i + 1) * ROWS, j * LANES : (j + 1) * LANES
            ]


def unspread(src_ref, dst_ref, count, sub):
    for i in range(count // ROWS):
        for j in range(sub):
            dst_ref[i * ROWS : (i + 1) * ROWS, j * LANES : (j + 1) * LANES] = src_ref[
                pl.ds(i * ROWS * sub + j, ROWS, stride=sub), :
            ]


def walk(lo, hi, step, state):
    groups = (hi - lo) // UNROLL

    def many(i, state):
        start = lo + i * UNROLL
        for k in range(UNROLL):
            state = step(start + k, state)
        return state

    state = lax.fori_loop(0, groups, many, state)
    return lax.fori_loop(lo + groups * UNROLL, hi, step, state)


def ends_kernel(
    lens_ref, own_ref, k_ref, v_ref, rate_ref, u_ref, end_ref, span_ref, base_ref, coef_ref,
    decay_sc, state_sc, *, tok, sub, poles, count, chunk,
):
    rate = rate_ref[...]
    spread(jnp.exp(-rate), decay_sc, sub)

    def mix(i, _):
        start = pl.multiple_of(i * chunk, chunk)
        u = k_ref[pl.ds(start, chunk), :].astype(F32) * v_ref[pl.ds(start, chunk), :].astype(F32)
        spread(u, u_ref, sub, start * sub)
        return 0

    lax.fori_loop(0, tok // chunk, mix, 0)
    decay = [decay_sc[p * sub : (p + 1) * sub, :] for p in range(poles)]

    def step(t, state):
        u = u_ref[pl.ds(pl.multiple_of(t * sub, sub), sub), :]
        return tuple(d * s + u for d, s in zip(decay, state))

    base_ref[...] = jnp.zeros_like(base_ref)
    coef_ref[...] = jnp.zeros_like(coef_ref)
    span_ref[...] = jnp.zeros_like(span_ref)
    zero = tuple(jnp.zeros((sub, LANES), F32) for _ in range(poles))
    for r, (lo, hi, before, reaches, ends, steps) in enumerate(spans(lens_ref, count, tok)):

        @pl.when(hi > lo)
        def _():
            state = walk(lo, hi, step, zero)
            for p in range(poles):
                state_sc[p * sub : (p + 1) * sub, :] = state[p]

            @pl.when(hi == tok)
            def _():
                unspread(state_sc, end_ref, poles, sub)

            @pl.when(ends)
            def _():
                unspread(state_sc, base_ref.at[own_ref[r]], poles, sub)

            @pl.when(before & ends)
            def _():
                coef_ref[own_ref[r]] = jnp.exp(rate * -steps.astype(F32))

            @pl.when(before & (hi == tok))
            def _():
                span_ref[...] = jnp.exp(rate * -float(tok))


def conv_kernel(
    lens_ref, u_ref, q_ref, rate_ref, res_ref, gain_ref, in_ref, out_ref,
    decay_sc, res_sc, state_sc, gain_sc, conv_sc, *, tok, sub, poles, count, chunk,
):
    rate = rate_ref[...]
    spread(jnp.exp(-rate), decay_sc, sub)
    spread(res_ref[...] * jnp.sqrt(1.0 - jnp.exp(-2.0 * rate)), res_sc, sub)
    for j in range(sub):
        gain_sc[j : j + 1, :] = gain_ref[0:1, j * LANES : (j + 1) * LANES]
    decay = [decay_sc[p * sub : (p + 1) * sub, :] for p in range(poles)]
    scale = [res_sc[p * sub : (p + 1) * sub, :] for p in range(poles)]
    gain = gain_sc[...]

    def step(t, state):
        rows = pl.ds(pl.multiple_of(t * sub, sub), sub)
        u = u_ref[rows, :]
        state = tuple(d * s + u for d, s in zip(decay, state))
        terms = [gain * u] + [c * s for c, s in zip(scale, state)]
        while len(terms) > 1:
            terms = [a + b for a, b in zip(terms[::2], terms[1::2])] + (
                [terms[-1]] if len(terms) % 2 else []
            )
        conv_sc[rows, :] = terms[0]
        return state

    for lo, hi, before, reaches, ends, steps in spans(lens_ref, count, tok):

        @pl.when(hi > lo)
        def _():
            @pl.when(before)
            def _():
                spread(in_ref[...], state_sc, sub)

            @pl.when(jnp.logical_not(before))
            def _():
                state_sc[...] = jnp.zeros_like(state_sc)

            state = tuple(state_sc[p * sub : (p + 1) * sub, :] for p in range(poles))
            walk(lo, hi, step, state)

    def gate(i, _):
        start = pl.multiple_of(i * chunk, chunk)
        rows = pl.ds(start, chunk)
        for j in range(sub):
            lanes = slice(j * LANES, (j + 1) * LANES)
            conv = conv_sc[pl.ds(start * sub + j, chunk, stride=sub), :]
            out_ref[rows, lanes] = (q_ref[rows, lanes].astype(F32) * conv).astype(out_ref.dtype)
        return 0

    lax.fori_loop(0, tok // chunk, gate, 0)


def shards(q_feat, k_feat, v_feat, pole_rate, residue, skip_gain, lengths, owners):
    tok, channels = q_feat.shape
    poles, count = pole_rate.shape[0], lengths.shape[0]
    slots = lax.axis_size("ctx")
    sub = min(ROWS, channels // LANES)
    width = sub * LANES
    tiles = channels // width
    sizes = dict(tok=tok, sub=sub, poles=poles, count=count, chunk=16)
    feat = pl.BlockSpec((tok, width), lambda i, *_: (0, i))
    pole = pl.BlockSpec((poles, width), lambda i, *_: (0, i))
    slot = pl.BlockSpec((slots, poles, width), lambda i, *_: (0, 0, i))
    flat = pl.BlockSpec((tok * sub, LANES), lambda i, *_: (i, 0))
    small = pltpu.VMEM((poles * sub, LANES), F32)
    elems = tok * channels
    mixed, end, span, base, coef = pl.pallas_call(
        functools.partial(ends_kernel, **sizes),
        grid_spec=pltpu.PrefetchScalarGridSpec(
            num_scalar_prefetch=2,
            grid=(tiles,),
            in_specs=[feat, feat, pole],
            out_specs=[flat, pole, pole, slot, slot],
            scratch_shapes=[small, small],
        ),
        out_shape=[
            jax.ShapeDtypeStruct((tiles * tok * sub, LANES), F32),
            jax.ShapeDtypeStruct((poles, channels), F32),
            jax.ShapeDtypeStruct((poles, channels), F32),
            jax.ShapeDtypeStruct((slots, poles, channels), F32),
            jax.ShapeDtypeStruct((slots, poles, channels), F32),
        ],
        cost_estimate=pl.CostEstimate(
            flops=2 * poles * elems, bytes_accessed=8 * elems, transcendentals=0
        ),
        name="ends",
    )(lengths, owners, k_feat, v_feat, pole_rate)

    longest = tok * slots // 2
    hops = min((longest - 2) // tok + 1, slots - 1)
    route = [(i, i + 1) for i in range(slots - 1)]
    incoming = lax.ppermute(end, "ctx", route)
    for _ in range(hops - 1):
        incoming = lax.ppermute(span * incoming + end, "ctx", route)
    slotted = base + coef * incoming[None]
    received = lax.all_to_all(
        slotted.reshape(slots, 1, poles, channels), "ctx", split_axis=0, concat_axis=0, tiled=True
    )
    decode_state = jnp.sum(received, axis=0)

    mixed_out = pl.pallas_call(
        functools.partial(conv_kernel, **sizes),
        grid_spec=pltpu.PrefetchScalarGridSpec(
            num_scalar_prefetch=1,
            grid=(tiles,),
            in_specs=[
                flat, feat, pole, pole, pl.BlockSpec((1, width), lambda i, *_: (0, i)), pole
            ],
            out_specs=feat,
            scratch_shapes=[
                small, small, small, pltpu.VMEM((sub, LANES), F32),
                pltpu.VMEM((tok * sub, LANES), F32),
            ],
        ),
        out_shape=jax.ShapeDtypeStruct((tok, channels), q_feat.dtype),
        cost_estimate=pl.CostEstimate(
            flops=8 * poles * elems, bytes_accessed=8 * elems, transcendentals=0
        ),
        name="conv",
    )(lengths, mixed, q_feat, pole_rate, residue, skip_gain[None, :], incoming)
    return mixed_out, decode_state


def solution(mesh):
    tokens = P(("groups", "ctx"), "chan")
    return jax.shard_map(
        shards,
        mesh=mesh,
        in_specs=(
            tokens, tokens, tokens, P(None, "chan"), P(None, "chan"), P("chan"),
            P("groups"), P("groups"),
        ),
        out_specs=(tokens, P(("groups", "ctx"), None, "chan")),
        check_vma=False,
    )
```

time: 432 us -> 50 us (0.12)
  matrix products: 167 us -> 0 us
  other arithmetic: 141 us -> 3.81 us
  local copies, waits for them, and re-layouts: 64.3 us -> 0.01 us
  loops' own time: 27.7 us -> 0 us
  Pallas kernels: 0 us -> 24.5 us
  starting transfers between devices: 19.5 us -> 15.1 us
    dot_general x34 -> x0, matrix products: 167 us -> none  [the longest x16 110 us: block_step(): jnp.einsum('ts,tsc,sc->tc', same_seg, toeplitz, u_block, precision=HIGH)]
    dot_general x32 -> x0, other arithmetic: 58 us -> none  [the longest x16 46.1 us: block_step(): jnp.einsum('psc,sc->pc', decay_back, weighted, precision=HIGH)]
    convert_element_type x52 -> x0, other arithmetic: 30.3 us -> none  [the longest x16 11.2 us: block_step(): live_mask = (seg_block == carry_seg).astype(jnp.float32)]
    another operation x2 -> x0, loops' own time: 27.7 us -> none  [the longest x1 27.6 us: shards(): lax.scan(block_step, init_carry, block_inputs)]
    pallas_call x0 -> x2, Pallas kernels: none -> 24.5 us  [the longest x1 14.6 us: shards(): pl.pallas_call(functools.partial(conv_kernel, **sizes), grid_spec=pltpu.P...]
    while x32 -> x0, other arithmetic: 18 us -> none
    dynamic_update_slice x16 -> x0, other arithmetic: 13.3 us -> none  [shards(): lax.scan(block_step, init_carry, block_inputs)]
    exp x1 -> x0, local copies, waits for them, and re-layouts: 12.6 us -> none  [shards(): jnp.exp(-pole_rate[:, None, :] * (step_float[None, :, None] + 1.0))]
  transfers between devices with their start and end apart: 4 -> 3, of which waited for: 3 -> 2; matrix products, arithmetic and copies ran while one was open for 14% -> 0% of each run, Pallas kernels for 0% -> 29%
where the time goes in v1:
time: 50 us; the launch traced here: 49.7 us
  Pallas kernels  24.5 us (49%)
  starting transfers between devices  15.1 us (30%)
  waiting for transfers between devices  5.54 us (11%)
  other arithmetic  3.81 us (8%)
  between operations  0.65 us (1%)
    pallas_call x1, Pallas kernels, shards(): pl.pallas_call(functools.partial(conv_kernel, **sizes), grid_spec=pltpu.P...  14.6 us
    pallas_call x1, Pallas kernels, shards(): pl.pallas_call(functools.partial(ends_kernel, **sizes), grid_spec=pltpu.P...  9.92 us
    all_to_all x1, starting transfers between devices, shards(): lax.all_to_all(slotted.reshape(slots, 1, poles, channels), 'ctx', split_a...  5.43 us
    ppermute x1, starting transfers between devices, shards(): incoming = lax.ppermute(end, 'ctx', route)  5.43 us
    ppermute x1, starting transfers between devices, shards(): incoming = lax.ppermute(span * incoming + end, 'ctx', route)  4.29 us
    ppermute x1, waiting for transfers between devices, shards(): incoming = lax.ppermute(end, 'ctx', route)  3.05 us
    ppermute x1, waiting for transfers between devices, shards(): incoming = lax.ppermute(span * incoming + end, 'ctx', route)  2.5 us
    reshape x1, other arithmetic, shards(): slotted.reshape(slots, 1, poles, channels)  2.13 us
  transfers between devices with their start and end apart: 3, of which 2 were waited for; matrix products, arithmetic and copies ran while one was open for 0% of the time, Pallas kernels for 29%

profile of v1, /device:TPU:0, one launch (start us, length us, event | category | flops | bytes accessed | tf_op | source)
XLA Modules:
  0.0 49.7 jit_solution(776412499652991723)
XLA Ops:
  0.6 9.9 %ends.1 = (f32[8192,128]{1,0:T(8,128)}, f32[16,2048]{1,0:T(8,128)}, f32[16,2048]{1,0:T(8,128)}, f32[4,16,2048]{2,1,0:T(8,128)}, f32[4,16,2048]{2,1,0:T(8,128)}) custom-call(s32[4]{0:T(128)} %lens_ref.3, s32[4]{0:T(128)} %own_ref.1, bf16[512,2048]{1,0:T(8,128)(2,1)} %k_ref.1, bf16[512,2048]{1,0:T(8,128)(2,1)} %v_ref.1, f32[16,2048]{1,0:T(8,128)} %rate_ref.3), custom_call_target="tpu_custom_call" | custom-call | flops 33554432 | bytes 8388608 | tf_op jit(solution)/shard_map/ends/pallas_call | solution.py:174
  10.6 5.4 %collective-permute-start = (f32[16,2048]{1,0:T(8,128)}, f32[16,2048]{1,0:T(8,128)S(1)}, u32[]{:S(2)}, u32[]{:S(2)}) collective-permute-start(f32[16,2048]{1,0:T(8,128)} %get-tuple-element.9), channel_id=1, source_target_pairs={{0,4},{4,8},{8,12},{1,5},{5,9},{9,13},{2,6},{6,10},{10,14},{3,7},{... | collective-permute-start | bytes 393224 | tf_op jit(solution)/shard_map/ppermute | solution.py:199
  16.0 3.0 %collective-permute-done = f32[16,2048]{1,0:T(8,128)S(1)} collective-permute-done((f32[16,2048]{1,0:T(8,128)}, f32[16,2048]{1,0:T(8,128)S(1)}, u32[]{:S(2)}, u32[]{:S(2)}) %collective-permute-start) | collective-permute-done | bytes 131104 | tf_op jit(solution)/shard_map/ppermute | solution.py:199
  19.0 1.0 %multiply_add_fusion = f32[16,2048]{1,0:T(8,128)S(1)} fusion(f32[16,2048]{1,0:T(8,128)} %get-tuple-element.9, f32[16,2048]{1,0:T(8,128)} %get-tuple-element.8, f32[16,2048]{1,0:T(8,128)S(1)} %collective-permute-done), kind=kLoop, calls=%fused_computation.1 | loop fusion | flops 65536 | bytes 524288 | tf_op jit(solution)/shard_map/add | solution.py:201
  20.0 4.3 %collective-permute-start.1 = (f32[16,2048]{1,0:T(8,128)S(1)}, f32[16,2048]{1,0:T(8,128)S(1)}, u32[]{:S(2)}, u32[]{:S(2)}) collective-permute-start(f32[16,2048]{1,0:T(8,128)S(1)} %multiply_add_fusion), channel_id=1, source_target_pairs={{0,4},{4,8},{8,12},{1,5},{5,9},{9,13},{2,6},{6,10},{10,14},{3,7},{... | collective-permute-start | bytes 393224 | tf_op jit(solution)/shard_map/ppermute | solution.py:201
  24.3 2.5 %collective-permute-done.1.in_ref = f32[16,2048]{1,0:T(8,128)S(1)} collective-permute-done((f32[16,2048]{1,0:T(8,128)S(1)}, f32[16,2048]{1,0:T(8,128)S(1)}, u32[]{:S(2)}, u32[]{:S(2)}) %collective-permute-start.1) | collective-permute-done | bytes 131104 | tf_op jit(solution)/shard_map/ppermute | solution.py:201
  26.8 0.0 copy-start
  26.8 2.1 %add_bitcast_fusion = f32[4,1,16,2048]{3,2,1,0:T(8,128)} fusion(f32[4,16,2048]{2,1,0:T(8,128)} %get-tuple-element.10, f32[4,16,2048]{2,1,0:T(8,128)} %get-tuple-element.11, f32[16,2048]{1,0:T(8,128)S(1)} %collective-permute-done.1.in_ref), kind=kLoop, calls=%fused_computation | loop fusion | flops 262144 | bytes 1703936 | tf_op jit(solution)/shard_map/reshape | solution.py:204
  28.9 5.4 %all-to-all-start = ((f32[4,1,16,2048]{3,2,1,0:T(8,128)}), f32[4,1,16,2048]{3,2,1,0:T(8,128)S(1)}, u32[]{:S(2)}, u32[]{:S(2)}) async-start(f32[4,1,16,2048]{3,2,1,0:T(8,128)} %add_bitcast_fusion), calls=%async_computation | async-start | bytes 1048576 | tf_op jit(solution)/shard_map/all_to_all | solution.py:203
  34.4 0.0 copy-done
  34.4 14.6 %conv.1 = bf16[512,2048]{1,0:T(8,128)(2,1)} custom-call(s32[4]{0:T(128)} %lens_ref.3, f32[8192,128]{1,0:T(8,128)} %get-tuple-element.7.u_ref, bf16[512,2048]{1,0:T(8,128)(2,1)} %q_ref.1, f32[16,2048]{1,0:T(8,128)} %rate_ref.3, f32[16,2048]{1,0:T(8,128)} %res_ref.1, f32[1,2048]{1,0:T(1,128)} %bitcast.7, f32[16,2048]{1,0:T(8,128)} %copy-done), custom_call_target="tpu_custom_call" | custom-call | flops 134217728 | bytes 8388608 | tf_op jit(solution)/shard_map/conv/pallas_call | solution.py:208
  49.0 0.0 all-to-all-done
  49.0 0.7 %reduce_sum.11 = f32[16,2048]{1,0:T(8,128)} reduce(f32[4,1,16,2048]{3,2,1,0:T(8,128)S(1)} %all-to-all-done, f32[]{:T(128)} %constant.0.clone.1), dimensions={0,1}, to_apply=%region_0.0 | reduce | flops 98304 | bytes 655364 | tf_op jit(solution)/shard_map/reduce_sum | solution.py:206
Async XLA Ops:
  10.6 8.5 %collective-permute-start = (f32[16,2048]{1,0:T(8,128)}, f32[16,2048]{1,0:T(8,128)S(1)}, u32[]{:S(2)}, u32[]{:S(2)}) collective-permute-start(f32[16,2048]{1,0:T(8,128)} %get-tuple-element.9), channel_id=1, source_target_pairs={{0,4},{4,8},{8,12},{1,5},{5,9},{9,13},{2,6},{6,10},{10,14},{3,7},{... | collective-permute-start | bytes 393224 | tf_op jit(solution)/shard_map/ppermute | solution.py:199
  20.0 6.8 %collective-permute-start.1 = (f32[16,2048]{1,0:T(8,128)S(1)}, f32[16,2048]{1,0:T(8,128)S(1)}, u32[]{:S(2)}, u32[]{:S(2)}) collective-permute-start(f32[16,2048]{1,0:T(8,128)S(1)} %multiply_add_fusion), channel_id=1, source_target_pairs={{0,4},{4,8},{8,12},{1,5},{5,9},{9,13},{2,6},{6,10},{10,14},{3,7},{... | collective-permute-start | bytes 393224 | tf_op jit(solution)/shard_map/ppermute | solution.py:201
  26.8 7.6 %copy-start = (f32[16,2048]{1,0:T(8,128)}, f32[16,2048]{1,0:T(8,128)S(1)}, u32[]{:S(2)}) copy-start(f32[16,2048]{1,0:T(8,128)S(1)} %collective-permute-done.1.in_ref) | copy-start | bytes 393220
  28.9 20.1 %all-to-all-start = ((f32[4,1,16,2048]{3,2,1,0:T(8,128)}), f32[4,1,16,2048]{3,2,1,0:T(8,128)S(1)}, u32[]{:S(2)}, u32[]{:S(2)}) async-start(f32[4,1,16,2048]{3,2,1,0:T(8,128)} %add_bitcast_fusion), calls=%async_computation | async-start | bytes 1048576 | tf_op jit(solution)/shard_map/all_to_all | solution.py:203

commit v2 on v1

--- a/solution.py
+++ b/solution.py
@@ -105,8 +105,104 @@
                 span_ref[...] = jnp.exp(rate * -float(tok))
 
 
+def relay_kernel(
+    end_ref, span_ref, base_ref, coef_ref, in_ref, got_ref,
+    arrived, passed, slotted, landed, sent_sem, come_sem, give_sem, take_sem,
+    *, hops, parts,
+):
+    slots, _, channels = base_ref.shape
+    width = channels // parts
+    me = lax.axis_index("ctx")
+    barrier = pltpu.get_barrier_semaphore()
+    peers = [lax.rem(me + j, slots) for j in range(1, slots)]
+    for peer in peers:
+        pl.semaphore_signal(
+            barrier, inc=1, device_id={"ctx": peer}, device_id_type=pl.DeviceIdType.MESH
+        )
+    pl.semaphore_wait(barrier, slots - 1)
+
+    def lanes(part):
+        return pl.ds(part * width, width)
+
+    def pass_on(hop, part):
+        source = end_ref if hop == 0 else passed.at[hop - 1]
+        return pltpu.make_async_remote_copy(
+            src_ref=source.at[:, lanes(part)],
+            dst_ref=arrived.at[hop, :, lanes(part)],
+            send_sem=sent_sem.at[hop, part],
+            recv_sem=come_sem.at[hop, part],
+            device_id={"ctx": lax.rem(me + 1, slots)},
+            device_id_type=pl.DeviceIdType.MESH,
+        )
+
+    def give(j, part):
+        return pltpu.make_async_remote_copy(
+            src_ref=slotted.at[j - 1, :, lanes(part)],
+            dst_ref=landed.at[j - 1, :, lanes(part)],
+            send_sem=give_sem.at[j - 1, part],
+            recv_sem=take_sem.at[j - 1, part],
+            device_id={"ctx": peers[j - 1]},
+            device_id_type=pl.DeviceIdType.MESH,
+        )
+
+    @pl.when(me == 0)
+    def _():
+        arrived[...] = jnp.zeros_like(arrived)
+
+    for hop in range(hops):
+        for part in range(parts):
+            if hop:
+
+                @pl.when(me > 0)
+                def _():
+                    pass_on(hop - 1, part).wait_recv()
+
+                at = lanes(part)
+                passed[hop - 1, :, at] = (
+                    span_ref[:, at] * arrived[hop - 1, :, at] + end_ref[:, at]
+                )
+
+            @pl.when(me < slots - 1)
+            def _():
+                pass_on(hop, part).start()
+
+    for part in range(parts):
+
+        @pl.when(me > 0)
+        def _():
+            pass_on(hops - 1, part).wait_recv()
+
+        at = lanes(part)
+        incoming = arrived[hops - 1, :, at]
+        in_ref[:, at] = incoming
+        for j in range(1, slots):
+            slotted[j - 1, :, at] = (
+                base_ref[peers[j - 1], :, at] + coef_ref[peers[j - 1], :, at] * incoming
+            )
+            give(j, part).start()
+        got_ref[:, at] = base_ref[me, :, at] + coef_ref[me, :, at] * incoming
+
+    for part in range(parts):
+        at = lanes(part)
+        for j in range(1, slots):
+            give(j, part).wait_recv()
+        total = got_ref[:, at]
+        for j in range(1, slots):
+            total += landed[j - 1, :, at]
+        got_ref[:, at] = total
+    for part in range(parts):
+        for j in range(1, slots):
+            give(j, part).wait_send()
+
+    @pl.when(me < slots - 1)
+    def _():
+        for hop in range(hops):
+            for part in range(parts):
+                pass_on(hop, part).wait_send()
+
+
 def conv_kernel(
-    lens_ref, u_ref, q_ref, rate_ref, res_ref, gain_ref, in_ref, out_ref,
+    lens_ref, u_ref, q_ref, rate_ref, res_ref, gain_ref, in_ref, got_ref, out_ref, kept_ref,
     decay_sc, res_sc, state_sc, gain_sc, conv_sc, *, tok, sub, poles, count, chunk,
 ):
     rate = rate_ref[...]
@@ -114,6 +210,7 @@
     spread(res_ref[...] * jnp.sqrt(1.0 - jnp.exp(-2.0 * rate)), res_sc, sub)
     for j in range(sub):
         gain_sc[j : j + 1, :] = gain_ref[0:1, j * LANES : (j + 1) * LANES]
+    kept_ref[0] = got_ref[...]
     decay = [decay_sc[p * sub : (p + 1) * sub, :] for p in range(poles)]
     scale = [res_sc[p * sub : (p + 1) * sub, :] for p in range(poles)]
     gain = gain_sc[...]
@@ -195,36 +292,49 @@
 
     longest = tok * slots // 2
     hops = min((longest - 2) // tok + 1, slots - 1)
-    route = [(i, i + 1) for i in range(slots - 1)]
-    incoming = lax.ppermute(end, "ctx", route)
-    for _ in range(hops - 1):
-        incoming = lax.ppermute(span * incoming + end, "ctx", route)
-    slotted = base + coef * incoming[None]
-    received = lax.all_to_all(
-        slotted.reshape(slots, 1, poles, channels), "ctx", split_axis=0, concat_axis=0, tiled=True
-    )
-    decode_state = jnp.sum(received, axis=0)
-
-    mixed_out = pl.pallas_call(
+    parts = max(1, min(4, channels // LANES))
+    dma = pltpu.SemaphoreType.DMA
+    incoming, got = pl.pallas_call(
+        functools.partial(relay_kernel, hops=hops, parts=parts),
+        in_specs=[pl.BlockSpec(memory_space=pltpu.VMEM)] * 4,
+        out_specs=[pl.BlockSpec(memory_space=pltpu.VMEM)] * 2,
+        out_shape=[jax.ShapeDtypeStruct((poles, channels), F32)] * 2,
+        scratch_shapes=[
+            pltpu.VMEM((hops, poles, channels), F32),
+            pltpu.VMEM((max(hops - 1, 1), poles, channels), F32),
+            pltpu.VMEM((slots - 1, poles, channels), F32),
+            pltpu.VMEM((slots - 1, poles, channels), F32),
+            dma((hops, parts)), dma((hops, parts)),
+            dma((slots - 1, parts)), dma((slots - 1, parts)),
+        ],
+        compiler_params=pltpu.CompilerParams(collective_id=0, has_side_effects=True),
+        name="relay",
+    )(end, span, base, coef)
+
+    mixed_out, decode_state = pl.pallas_call(
         functools.partial(conv_kernel, **sizes),
         grid_spec=pltpu.PrefetchScalarGridSpec(
             num_scalar_prefetch=1,
             grid=(tiles,),
             in_specs=[
-                flat, feat, pole, pole, pl.BlockSpec((1, width), lambda i, *_: (0, i)), pole
+                flat, feat, pole, pole, pl.BlockSpec((1, width), lambda i, *_: (0, i)), pole,
+                pole,
             ],
-            out_specs=feat,
+            out_specs=[feat, pl.BlockSpec((1, poles, width), lambda i, *_: (0, 0, i))],
             scratch_shapes=[
                 small, small, small, pltpu.VMEM((sub, LANES), F32),
                 pltpu.VMEM((tok * sub, LANES), F32),
             ],
         ),
-        out_shape=jax.ShapeDtypeStruct((tok, channels), q_feat.dtype),
+        out_shape=[
+            jax.ShapeDtypeStruct((tok, channels), q_feat.dtype),
+            jax.ShapeDtypeStruct((1, poles, channels), F32),
+        ],
         cost_estimate=pl.CostEstimate(
             flops=8 * poles * elems, bytes_accessed=8 * elems, transcendentals=0
         ),
         name="conv",
-    )(lengths, mixed, q_feat, pole_rate, residue, skip_gain[None, :], incoming)
+    )(lengths, mixed, q_feat, pole_rate, residue, skip_gain[None, :], incoming, got)
     return mixed_out, decode_state
 
 

time: 50 us -> 50.4 us (level)
  Pallas kernels: 24.5 us -> 49.6 us
  starting transfers between devices: 15.1 us -> 0 us
  waiting for transfers between devices: 5.54 us -> 0 us
  other arithmetic: 3.81 us -> 0 us
    pallas_call x0 -> x1, Pallas kernels: none -> 24.9 us  [shards(): pl.pallas_call(functools.partial(relay_kernel, hops=hops, parts=parts), i...]
    ppermute x2 -> x0, starting transfers between devices: 9.71 us -> none  [the longest x1 5.43 us: shards(): incoming = lax.ppermute(end, 'ctx', route)]
    ppermute x2 -> x0, waiting for transfers between devices: 5.54 us -> none  [the longest x1 3.05 us: shards(): incoming = lax.ppermute(end, 'ctx', route)]
    all_to_all x1 -> x0, starting transfers between devices: 5.43 us -> none  [shards(): lax.all_to_all(slotted.reshape(slots, 1, poles, channels), 'ctx', split_a...]
    reshape x1 -> x0, other arithmetic: 2.13 us -> none  [shards(): slotted.reshape(slots, 1, poles, channels)]
    add x1 -> x0, other arithmetic: 1 us -> none  [shards(): incoming = lax.ppermute(span * incoming + end, 'ctx', route)]
    reduce_sum x1 -> x0, other arithmetic: 0.68 us -> none  [shards(): decode_state = jnp.sum(received, axis=0)]
  transfers between devices with their start and end apart: 3 -> 0, of which waited for: 2 -> 0; matrix products, arithmetic and copies ran while one was open for 0% -> 0% of each run, Pallas kernels for 29% -> 0%
where the time goes in v2:
time: 50.4 us; the launch traced here: 50.3 us
  Pallas kernels  49.6 us (98%)
  between operations  0.64 us (1%)
    pallas_call x1, Pallas kernels, shards(): pl.pallas_call(functools.partial(relay_kernel, hops=hops, parts=parts), i...  24.9 us
    pallas_call x1, Pallas kernels, shards(): pl.pallas_call(functools.partial(conv_kernel, **sizes), grid_spec=pltpu.P...  14.7 us
    pallas_call x1, Pallas kernels, shards(): pl.pallas_call(functools.partial(ends_kernel, **sizes), grid_spec=pltpu.P...  10 us

profile of v2, /device:TPU:0, one launch (start us, length us, event | category | flops | bytes accessed | tf_op | source)
XLA Modules:
  0.0 50.3 jit_solution(15437141395419132645)
XLA Ops:
  0.6 10.0 %ends.1 = (f32[8192,128]{1,0:T(8,128)}, f32[16,2048]{1,0:T(8,128)}, f32[16,2048]{1,0:T(8,128)}, f32[4,16,2048]{2,1,0:T(8,128)}, f32[4,16,2048]{2,1,0:T(8,128)}) custom-call(s32[4]{0:T(128)} %lens_ref.3, s32[4]{0:T(128)} %own_ref.1, bf16[512,2048]{1,0:T(8,128)(2,1)} %k_ref.1, bf16[512,2048]{1,0:T(8,128)(2,1)} %v_ref.1, f32[16,2048]{1,0:T(8,128)} %rate_ref.3), custom_call_target="tpu_custom_call" | custom-call | flops 33554432 | bytes 8388608 | tf_op jit(solution)/shard_map/ends/pallas_call | solution.py:271
  10.6 24.9 %relay.1 = (f32[16,2048]{1,0:T(8,128)}, f32[16,2048]{1,0:T(8,128)}) custom-call(f32[16,2048]{1,0:T(8,128)} %get-tuple-element.10.end_ref, f32[16,2048]{1,0:T(8,128)} %get-tuple-element.11.span_ref, f32[4,16,2048]{2,1,0:T(8,128)} %get-tuple-element.12.base_ref, f32[4,16,2048]{2,1,0:T(8,128)} %get-tuple-element.13.coef_ref), custom_call_target="tpu_custom_call" | custom-call | tf_op jit(solution)/shard_map/relay/pallas_call | solution.py:297
  35.5 14.7 %conv.1 = (bf16[512,2048]{1,0:T(8,128)(2,1)}, f32[1,16,2048]{2,1,0:T(8,128)}) custom-call(s32[4]{0:T(128)} %lens_ref.3, f32[8192,128]{1,0:T(8,128)} %get-tuple-element.9.u_ref, bf16[512,2048]{1,0:T(8,128)(2,1)} %q_ref.1, f32[16,2048]{1,0:T(8,128)} %rate_ref.3, f32[16,2048]{1,0:T(8,128)} %res_ref.1, f32[1,2048]{1,0:T(1,128)} %bitcast.1, ...), custom_call_target="tpu_custom_call" | custom-call | flops 134217728 | bytes 8388608 | tf_op jit(solution)/shard_map/conv/pallas_call | solution.py:314

commit v3 on v2

--- a/solution.py
+++ b/solution.py
@@ -107,19 +107,18 @@
 
 def relay_kernel(
     end_ref, span_ref, base_ref, coef_ref, in_ref, got_ref,
-    arrived, passed, slotted, landed, sent_sem, come_sem, give_sem, take_sem,
+    arrived, passed, sent_sem, come_sem,
     *, hops, parts,
 ):
     slots, _, channels = base_ref.shape
     width = channels // parts
     me = lax.axis_index("ctx")
     barrier = pltpu.get_barrier_semaphore()
-    peers = [lax.rem(me + j, slots) for j in range(1, slots)]
-    for peer in peers:
+    for peer in (lax.rem(me + 1, slots), lax.rem(me + slots - 1, slots)):
         pl.semaphore_signal(
             barrier, inc=1, device_id={"ctx": peer}, device_id_type=pl.DeviceIdType.MESH
         )
-    pl.semaphore_wait(barrier, slots - 1)
+    pl.semaphore_wait(barrier, 2)
 
     def lanes(part):
         return pl.ds(part * width, width)
@@ -135,16 +134,6 @@
             device_id_type=pl.DeviceIdType.MESH,
         )
 
-    def give(j, part):
-        return pltpu.make_async_remote_copy(
-            src_ref=slotted.at[j - 1, :, lanes(part)],
-            dst_ref=landed.at[j - 1, :, lanes(part)],
-            send_sem=give_sem.at[j - 1, part],
-            recv_sem=take_sem.at[j - 1, part],
-            device_id={"ctx": peers[j - 1]},
-            device_id_type=pl.DeviceIdType.MESH,
-        )
-
     @pl.when(me == 0)
     def _():
         arrived[...] = jnp.zeros_like(arrived)
@@ -175,24 +164,8 @@
         at = lanes(part)
         incoming = arrived[hops - 1, :, at]
         in_ref[:, at] = incoming
-        for j in range(1, slots):
-            slotted[j - 1, :, at] = (
-                base_ref[peers[j - 1], :, at] + coef_ref[peers[j - 1], :, at] * incoming
-            )
-            give(j, part).start()
-        got_ref[:, at] = base_ref[me, :, at] + coef_ref[me, :, at] * incoming
-
-    for part in range(parts):
-        at = lanes(part)
-        for j in range(1, slots):
-            give(j, part).wait_recv()
-        total = got_ref[:, at]
-        for j in range(1, slots):
-            total += landed[j - 1, :, at]
-        got_ref[:, at] = total
-    for part in range(parts):
-        for j in range(1, slots):
-            give(j, part).wait_send()
+        for q in range(slots):
+            got_ref[q, :, at] = base_ref[q, :, at] + coef_ref[q, :, at] * incoming
 
     @pl.when(me < slots - 1)
     def _():
@@ -202,7 +175,7 @@
 
 
 def conv_kernel(
-    lens_ref, u_ref, q_ref, rate_ref, res_ref, gain_ref, in_ref, got_ref, out_ref, kept_ref,
+    lens_ref, u_ref, q_ref, rate_ref, res_ref, gain_ref, in_ref, out_ref,
     decay_sc, res_sc, state_sc, gain_sc, conv_sc, *, tok, sub, poles, count, chunk,
 ):
     rate = rate_ref[...]
@@ -210,7 +183,6 @@
     spread(res_ref[...] * jnp.sqrt(1.0 - jnp.exp(-2.0 * rate)), res_sc, sub)
     for j in range(sub):
         gain_sc[j : j + 1, :] = gain_ref[0:1, j * LANES : (j + 1) * LANES]
-    kept_ref[0] = got_ref[...]
     decay = [decay_sc[p * sub : (p + 1) * sub, :] for p in range(poles)]
     scale = [res_sc[p * sub : (p + 1) * sub, :] for p in range(poles)]
     gain = gain_sc[...]
@@ -294,47 +266,48 @@
     hops = min((longest - 2) // tok + 1, slots - 1)
     parts = max(1, min(4, channels // LANES))
     dma = pltpu.SemaphoreType.DMA
-    incoming, got = pl.pallas_call(
+    incoming, slotted = pl.pallas_call(
         functools.partial(relay_kernel, hops=hops, parts=parts),
         in_specs=[pl.BlockSpec(memory_space=pltpu.VMEM)] * 4,
         out_specs=[pl.BlockSpec(memory_space=pltpu.VMEM)] * 2,
-        out_shape=[jax.ShapeDtypeStruct((poles, channels), F32)] * 2,
+        out_shape=[
+            jax.ShapeDtypeStruct((poles, channels), F32),
+            jax.ShapeDtypeStruct((slots, poles, channels), F32),
+        ],
         scratch_shapes=[
             pltpu.VMEM((hops, poles, channels), F32),
             pltpu.VMEM((max(hops - 1, 1), poles, channels), F32),
-            pltpu.VMEM((slots - 1, poles, channels), F32),
-            pltpu.VMEM((slots - 1, poles, channels), F32),
             dma((hops, parts)), dma((hops, parts)),
-            dma((slots - 1, parts)), dma((slots - 1, parts)),
         ],
         compiler_params=pltpu.CompilerParams(collective_id=0, has_side_effects=True),
         name="relay",
     )(end, span, base, coef)
 
-    mixed_out, decode_state = pl.pallas_call(
+    received = lax.all_to_all(
+        slotted.reshape(slots, 1, poles, channels), "ctx", split_axis=0, concat_axis=0, tiled=True
+    )
+    decode_state = jnp.sum(received, axis=0)
+
+    mixed_out = pl.pallas_call(
         functools.partial(conv_kernel, **sizes),
         grid_spec=pltpu.PrefetchScalarGridSpec(
             num_scalar_prefetch=1,
             grid=(tiles,),
             in_specs=[
-                flat, feat, pole, pole, pl.BlockSpec((1, width), lambda i, *_: (0, i)), pole,
-                pole,
+                flat, feat, pole, pole, pl.BlockSpec((1, width), lambda i, *_: (0, i)), pole
             ],
-            out_specs=[feat, pl.BlockSpec((1, poles, width), lambda i, *_: (0, 0, i))],
+            out_specs=feat,
             scratch_shapes=[
                 small, small, small, pltpu.VMEM((sub, LANES), F32),
                 pltpu.VMEM((tok * sub, LANES), F32),
             ],
         ),
-        out_shape=[
-            jax.ShapeDtypeStruct((tok, channels), q_feat.dtype),
-            jax.ShapeDtypeStruct((1, poles, channels), F32),
-        ],
+        out_shape=jax.ShapeDtypeStruct((tok, channels), q_feat.dtype),
         cost_estimate=pl.CostEstimate(
             flops=8 * poles * elems, bytes_accessed=8 * elems, transcendentals=0
         ),
         name="conv",
-    )(lengths, mixed, q_feat, pole_rate, residue, skip_gain[None, :], incoming, got)
+    )(lengths, mixed, q_feat, pole_rate, residue, skip_gain[None, :], incoming)
     return mixed_out, decode_state
 
 

time: 50.4 us -> 44.8 us (0.89)
  Pallas kernels: 49.6 us -> 37.8 us
  starting transfers between devices: 0 us -> 5.47 us
  other arithmetic: 0 us -> 0.68 us
    pallas_call x1, Pallas kernels: 24.9 us -> 13.1 us  [shards(): pl.pallas_call(functools.partial(relay_kernel, hops=hops, parts=parts), i...]
    all_to_all x0 -> x1, starting transfers between devices: none -> 5.47 us  [shards(): lax.all_to_all(slotted.reshape(slots, 1, poles, channels), 'ctx', split_a...]
    reduce_sum x0 -> x1, other arithmetic: none -> 0.68 us  [shards(): decode_state = jnp.sum(received, axis=0)]
  transfers between devices with their start and end apart: 0 -> 1, of which waited for: 0 -> 0; matrix products, arithmetic and copies ran while one was open for 0% -> 0% of each run, Pallas kernels for 0% -> 33%
where the time goes in v3:
time: 44.8 us; the launch traced here: 44.6 us
  Pallas kernels  37.8 us (84%)
  starting transfers between devices  5.47 us (12%)
  other arithmetic  0.68 us (2%)
  between operations  0.64 us (1%)
    pallas_call x1, Pallas kernels, shards(): pl.pallas_call(functools.partial(conv_kernel, **sizes), grid_spec=pltpu.P...  14.7 us
    pallas_call x1, Pallas kernels, shards(): pl.pallas_call(functools.partial(relay_kernel, hops=hops, parts=parts), i...  13.1 us
    pallas_call x1, Pallas kernels, shards(): pl.pallas_call(functools.partial(ends_kernel, **sizes), grid_spec=pltpu.P...  10 us
    all_to_all x1, starting transfers between devices, shards(): lax.all_to_all(slotted.reshape(slots, 1, poles, channels), 'ctx', split_a...  5.47 us
  transfers between devices with their start and end apart: 1, of which 0 were waited for; matrix products, arithmetic and copies ran while one was open for 0% of the time, Pallas kernels for 33%

profile of v3, /device:TPU:0, one launch (start us, length us, event | category | flops | bytes accessed | tf_op | source)
XLA Modules:
  0.0 44.6 jit_solution(6337076445541016167)
XLA Ops:
  0.6 10.0 %ends.1 = (f32[8192,128]{1,0:T(8,128)}, f32[16,2048]{1,0:T(8,128)}, f32[16,2048]{1,0:T(8,128)}, f32[4,16,2048]{2,1,0:T(8,128)}, f32[4,16,2048]{2,1,0:T(8,128)}) custom-call(s32[4]{0:T(128)} %lens_ref.3, s32[4]{0:T(128)} %own_ref.1, bf16[512,2048]{1,0:T(8,128)(2,1)} %k_ref.1, bf16[512,2048]{1,0:T(8,128)(2,1)} %v_ref.1, f32[16,2048]{1,0:T(8,128)} %rate_ref.3), custom_call_target="tpu_custom_call" | custom-call | flops 33554432 | bytes 8388608 | tf_op jit(solution)/shard_map/ends/pallas_call | solution.py:243
  10.6 13.1 %relay.1 = (f32[16,2048]{1,0:T(8,128)}, f32[4,16,2048]{2,1,0:T(8,128)}) custom-call(f32[16,2048]{1,0:T(8,128)} %get-tuple-element.10.end_ref, f32[16,2048]{1,0:T(8,128)} %get-tuple-element.11.span_ref, f32[4,16,2048]{2,1,0:T(8,128)} %get-tuple-element.12.base_ref, f32[4,16,2048]{2,1,0:T(8,128)} %get-tuple-element.13.coef_ref), custom_call_target="tpu_custom_call" | custom-call | tf_op jit(solution)/shard_map/relay/pallas_call | solution.py:269
  23.7 5.5 %all-to-all-start = ((f32[4,1,16,2048]{3,2,1,0:T(8,128)}), f32[4,1,16,2048]{3,2,1,0:T(8,128)S(1)}, u32[]{:S(2)}, u32[]{:S(2)}) async-start(f32[4,1,16,2048]{3,2,1,0:T(8,128)} %bitcast.5), calls=%async_computation | async-start | bytes 1048576 | tf_op jit(solution)/shard_map/all_to_all | solution.py:286
  29.2 14.7 %conv.1 = bf16[512,2048]{1,0:T(8,128)(2,1)} custom-call(s32[4]{0:T(128)} %lens_ref.3, f32[8192,128]{1,0:T(8,128)} %get-tuple-element.9.u_ref, bf16[512,2048]{1,0:T(8,128)(2,1)} %q_ref.1, f32[16,2048]{1,0:T(8,128)} %rate_ref.3, f32[16,2048]{1,0:T(8,128)} %res_ref.1, f32[1,2048]{1,0:T(1,128)} %bitcast.7, f32[16,2048]{1,0:T(8,128)} %get-tuple-element.14.in_ref), custom_call_target="tpu_custom_call" | custom-call | flops 134217728 | bytes 8388608 | tf_op jit(solution)/shard_map/conv/pallas_call | solution.py:291
  43.9 0.0 all-to-all-done
  43.9 0.7 %reduce_sum.11 = f32[16,2048]{1,0:T(8,128)} reduce(f32[4,1,16,2048]{3,2,1,0:T(8,128)S(1)} %all-to-all-done, f32[]{:T(128)} %constant.0.clone.1), dimensions={0,1}, to_apply=%region_0.0 | reduce | flops 98304 | bytes 655364 | tf_op jit(solution)/shard_map/reduce_sum | solution.py:289
Async XLA Ops:
  23.7 20.2 %all-to-all-start = ((f32[4,1,16,2048]{3,2,1,0:T(8,128)}), f32[4,1,16,2048]{3,2,1,0:T(8,128)S(1)}, u32[]{:S(2)}, u32[]{:S(2)}) async-start(f32[4,1,16,2048]{3,2,1,0:T(8,128)} %bitcast.5), calls=%async_computation | async-start | bytes 1048576 | tf_op jit(solution)/shard_map/all_to_all | solution.py:286

commit v4 on v2

--- a/solution.py
+++ b/solution.py
@@ -105,13 +105,17 @@
                 span_ref[...] = jnp.exp(rate * -float(tok))
 
 
-def relay_kernel(
-    end_ref, span_ref, base_ref, coef_ref, in_ref, got_ref,
-    arrived, passed, slotted, landed, sent_sem, come_sem, give_sem, take_sem,
-    *, hops, parts,
+def conv_kernel(
+    lens_ref, end_ref, span_ref, base_ref, coef_ref, rate_ref, res_ref, gain_ref, u_hbm, q_hbm,
+    out_hbm, got_ref,
+    arrived, passed, slotted, landed, decay_sc, res_sc, state_sc, gain_sc, conv_sc,
+    u_ref, q_ref, out_ref, sent_sem, come_sem, give_sem, take_sem, load_sem, store_sem,
+    *, hops, parts, tok, sub, poles, count, chunk, tiles,
 ):
     slots, _, channels = base_ref.shape
     width = channels // parts
+    wide = sub * LANES
+    rows_in = tok * sub
     me = lax.axis_index("ctx")
     barrier = pltpu.get_barrier_semaphore()
     peers = [lax.rem(me + j, slots) for j in range(1, slots)]
@@ -119,6 +123,17 @@
         pl.semaphore_signal(
             barrier, inc=1, device_id={"ctx": peer}, device_id_type=pl.DeviceIdType.MESH
         )
+    loads = []
+    for i in range(tiles):
+        flat, cols = pl.ds(i * rows_in, rows_in), pl.ds(i * wide, wide)
+        loads.append(
+            (
+                pltpu.make_async_copy(u_hbm.at[flat, :], u_ref.at[flat, :], load_sem.at[i, 0]),
+                pltpu.make_async_copy(q_hbm.at[:, cols], q_ref.at[:, cols], load_sem.at[i, 1]),
+            )
+        )
+        loads[i][0].start()
+        loads[i][1].start()
     pl.semaphore_wait(barrier, slots - 1)
 
     def lanes(part):
@@ -145,51 +160,130 @@
             device_id_type=pl.DeviceIdType.MESH,
         )
 
-    @pl.when(me == 0)
-    def _():
-        arrived[...] = jnp.zeros_like(arrived)
-
-    for hop in range(hops):
-        for part in range(parts):
-            if hop:
-
-                @pl.when(me > 0)
-                def _():
-                    pass_on(hop - 1, part).wait_recv()
-
-                at = lanes(part)
-                passed[hop - 1, :, at] = (
-                    span_ref[:, at] * arrived[hop - 1, :, at] + end_ref[:, at]
-                )
-
-            @pl.when(me < slots - 1)
-            def _():
-                pass_on(hop, part).start()
-
-    for part in range(parts):
-
+    def arrive(hop, part):
         @pl.when(me > 0)
         def _():
-            pass_on(hops - 1, part).wait_recv()
-
+            pass_on(hop, part).wait_recv()
+
+    def hop_on(hop, part):
+        if hop:
+            arrive(hop - 1, part)
+            at = lanes(part)
+            passed[hop - 1, :, at] = span_ref[:, at] * arrived[hop - 1, :, at] + end_ref[:, at]
+
+        @pl.when(me < slots - 1)
+        def _():
+            pass_on(hop, part).start()
+
+    def finish(part):
+        arrive(hops - 1, part)
         at = lanes(part)
         incoming = arrived[hops - 1, :, at]
-        in_ref[:, at] = incoming
         for j in range(1, slots):
             slotted[j - 1, :, at] = (
                 base_ref[peers[j - 1], :, at] + coef_ref[peers[j - 1], :, at] * incoming
             )
             give(j, part).start()
-        got_ref[:, at] = base_ref[me, :, at] + coef_ref[me, :, at] * incoming
+        got_ref[0, :, at] = base_ref[me, :, at] + coef_ref[me, :, at] * incoming
+
+    @pl.when(me == 0)
+    def _():
+        arrived[...] = jnp.zeros_like(arrived)
+
+    for hop in range(hops):
+        for part in range(parts):
+            hop_on(hop, part)
+
+    first = me * tok
+    offset = jnp.int32(0)
+    starts = []
+    for r in range(count):
+        starts.append(offset - first)
+        offset = offset + lens_ref[r]
+
+    def conv(i, begin, stop):
+        scale = [res_sc[p] for p in range(poles)]
+        gain = gain_sc[...]
+
+        def many(n, state):
+            for k in range(UNROLL):
+                t = n * UNROLL + k
+                keep = jnp.int32(1)
+                for at in starts:
+                    keep = keep - (t == at).astype(jnp.int32)
+                pick = jnp.maximum(keep, 0) * poles
+                rows = pl.ds(pl.multiple_of(t * sub, sub), sub)
+                u = u_ref[pl.ds(pl.multiple_of(i * rows_in + t * sub, sub), sub), :]
+                state = tuple(decay_sc[pick + p] * s + u for p, s in enumerate(state))
+                terms = [gain * u] + [c * s for c, s in zip(scale, state)]
+                while len(terms) > 1:
+                    terms = [a + b for a, b in zip(terms[::2], terms[1::2])] + (
+                        [terms[-1]] if len(terms) % 2 else []
+                    )
+                conv_sc[rows, :] = terms[0]
+            return state
+
+        state = tuple(state_sc[p] for p in range(poles))
+        state = lax.fori_loop(begin // UNROLL, stop // UNROLL, many, state)
+        for p in range(poles):
+            state_sc[p] = state[p]
+
+    def scatter(value, ref, base):
+        for p in range(poles):
+            for j in range(sub):
+                ref[base + p, j : j + 1, :] = value[p : p + 1, j * LANES : (j + 1) * LANES]
+
+    stores = []
+    per_tile = parts // tiles
+    for i in range(tiles):
+        cols = slice(i * wide, (i + 1) * wide)
+        rate = rate_ref[:, cols]
+        decay_sc[0:poles] = jnp.zeros((poles, sub, LANES), F32)
+        scatter(jnp.exp(-rate), decay_sc, poles)
+        scatter(res_ref[:, cols] * jnp.sqrt(1.0 - jnp.exp(-2.0 * rate)), res_sc, 0)
+        for j in range(sub):
+            at = i * wide + j * LANES
+            gain_sc[j : j + 1, :] = gain_ref[0:1, at : at + LANES]
+        if i == 0:
+            for part in range(per_tile):
+                finish(part)
+        scatter(arrived[hops - 1, :, cols], state_sc, 0)
+        loads[i][0].wait()
+        if i == 0 and tiles > 1:
+            conv(i, 0, tok // 4)
+            for part in range(per_tile, parts):
+                finish(part)
+            conv(i, tok // 4, tok)
+        else:
+            conv(i, 0, tok)
+        loads[i][1].wait()
+
+        def gate(n, _):
+            start = pl.multiple_of(n * chunk, chunk)
+            rows = pl.ds(start, chunk)
+            for j in range(sub):
+                at = slice(i * wide + j * LANES, i * wide + (j + 1) * LANES)
+                value = conv_sc[pl.ds(start * sub + j, chunk, stride=sub), :]
+                out_ref[rows, at] = (q_ref[rows, at].astype(F32) * value).astype(out_ref.dtype)
+            return 0
+
+        lax.fori_loop(0, tok // chunk, gate, 0)
+        stores.append(
+            pltpu.make_async_copy(
+                out_ref.at[:, pl.ds(i * wide, wide)], out_hbm.at[:, pl.ds(i * wide, wide)],
+                store_sem.at[i],
+            )
+        )
+        stores[i].start()
 
     for part in range(parts):
         at = lanes(part)
         for j in range(1, slots):
             give(j, part).wait_recv()
-        total = got_ref[:, at]
+        total = got_ref[0, :, at]
         for j in range(1, slots):
             total += landed[j - 1, :, at]
-        got_ref[:, at] = total
+        got_ref[0, :, at] = total
     for part in range(parts):
         for j in range(1, slots):
             give(j, part).wait_send()
@@ -200,58 +294,8 @@
             for part in range(parts):
                 pass_on(hop, part).wait_send()
 
-
-def conv_kernel(
-    lens_ref, u_ref, q_ref, rate_ref, res_ref, gain_ref, in_ref, got_ref, out_ref, kept_ref,
-    decay_sc, res_sc, state_sc, gain_sc, conv_sc, *, tok, sub, poles, count, chunk,
-):
-    rate = rate_ref[...]
-    spread(jnp.exp(-rate), decay_sc, sub)
-    spread(res_ref[...] * jnp.sqrt(1.0 - jnp.exp(-2.0 * rate)), res_sc, sub)
-    for j in range(sub):
-        gain_sc[j : j + 1, :] = gain_ref[0:1, j * LANES : (j + 1) * LANES]
-    kept_ref[0] = got_ref[...]
-    decay = [decay_sc[p * sub : (p + 1) * sub, :] for p in range(poles)]
-    scale = [res_sc[p * sub : (p + 1) * sub, :] for p in range(poles)]
-    gain = gain_sc[...]
-
-    def step(t, state):
-        rows = pl.ds(pl.multiple_of(t * sub, sub), sub)
-        u = u_ref[rows, :]
-        state = tuple(d * s + u for d, s in zip(decay, state))
-        terms = [gain * u] + [c * s for c, s in zip(scale, state)]
-        while len(terms) > 1:
-            terms = [a + b for a, b in zip(terms[::2], terms[1::2])] + (
-                [terms[-1]] if len(terms) % 2 else []
-            )
-        conv_sc[rows, :] = terms[0]
-        return state
-
-    for lo, hi, before, reaches, ends, steps in spans(lens_ref, count, tok):
-
-        @pl.when(hi > lo)
-        def _():
-            @pl.when(before)
-            def _():
-                spread(in_ref[...], state_sc, sub)
-
-            @pl.when(jnp.logical_not(before))
-            def _():
-                state_sc[...] = jnp.zeros_like(state_sc)
-
-            state = tuple(state_sc[p * sub : (p + 1) * sub, :] for p in range(poles))
-            walk(lo, hi, step, state)
-
-    def gate(i, _):
-        start = pl.multiple_of(i * chunk, chunk)
-        rows = pl.ds(start, chunk)
-        for j in range(sub):
-            lanes = slice(j * LANES, (j + 1) * LANES)
-            conv = conv_sc[pl.ds(start * sub + j, chunk, stride=sub), :]
-            out_ref[rows, lanes] = (q_ref[rows, lanes].astype(F32) * conv).astype(out_ref.dtype)
-        return 0
-
-    lax.fori_loop(0, tok // chunk, gate, 0)
+    for copy in stores:
+        copy.wait()
 
 
 def shards(q_feat, k_feat, v_feat, pole_rate, residue, skip_gain, lengths, owners):
@@ -292,49 +336,39 @@
 
     longest = tok * slots // 2
     hops = min((longest - 2) // tok + 1, slots - 1)
-    parts = max(1, min(4, channels // LANES))
+    parts = max(tiles, min(4, channels // LANES))
     dma = pltpu.SemaphoreType.DMA
-    incoming, got = pl.pallas_call(
-        functools.partial(relay_kernel, hops=hops, parts=parts),
-        in_specs=[pl.BlockSpec(memory_space=pltpu.VMEM)] * 4,
-        out_specs=[pl.BlockSpec(memory_space=pltpu.VMEM)] * 2,
-        out_shape=[jax.ShapeDtypeStruct((poles, channels), F32)] * 2,
+    vmem, hbm = pl.BlockSpec(memory_space=pltpu.VMEM), pl.BlockSpec(memory_space=pl.ANY)
+    mixed_out, decode_state = pl.pallas_call(
+        functools.partial(conv_kernel, hops=hops, parts=parts, tiles=tiles, **sizes),
+        in_specs=[pl.BlockSpec(memory_space=pltpu.SMEM)] + [vmem] * 7 + [hbm] * 2,
+        out_specs=[hbm, vmem],
+        out_shape=[
+            jax.ShapeDtypeStruct((tok, channels), q_feat.dtype),
+            jax.ShapeDtypeStruct((1, poles, channels), F32),
+        ],
         scratch_shapes=[
             pltpu.VMEM((hops, poles, channels), F32),
             pltpu.VMEM((max(hops - 1, 1), poles, channels), F32),
             pltpu.VMEM((slots - 1, poles, channels), F32),
             pltpu.VMEM((slots - 1, poles, channels), F32),
+            pltpu.VMEM((2 * poles, sub, LANES), F32),
+            pltpu.VMEM((poles, sub, LANES), F32),
+            pltpu.VMEM((poles, sub, LANES), F32),
+            pltpu.VMEM((sub, LANES), F32),
+            pltpu.VMEM((tok * sub, LANES), F32),
+            pltpu.VMEM((tiles * tok * sub, LANES), F32),
+            pltpu.VMEM((tok, channels), q_feat.dtype),
+            pltpu.VMEM((tok, channels), q_feat.dtype),
             dma((hops, parts)), dma((hops, parts)),
             dma((slots - 1, parts)), dma((slots - 1, parts)),
+            dma((tiles, 2)), dma((tiles,)),
         ],
         compiler_params=pltpu.CompilerParams(collective_id=0, has_side_effects=True),
-        name="relay",
-    )(end, span, base, coef)
-
-    mixed_out, decode_state = pl.pallas_call(
-        functools.partial(conv_kernel, **sizes),
-        grid_spec=pltpu.PrefetchScalarGridSpec(
-            num_scalar_prefetch=1,
-            grid=(tiles,),
-            in_specs=[
-                flat, feat, pole, pole, pl.BlockSpec((1, width), lambda i, *_: (0, i)), pole,
-                pole,
-            ],
-            out_specs=[feat, pl.BlockSpec((1, poles, width), lambda i, *_: (0, 0, i))],
-            scratch_shapes=[
-                small, small, small, pltpu.VMEM((sub, LANES), F32),
-                pltpu.VMEM((tok * sub, LANES), F32),
-            ],
-        ),
-        out_shape=[
-            jax.ShapeDtypeStruct((tok, channels), q_feat.dtype),
-            jax.ShapeDtypeStruct((1, poles, channels), F32),
-        ],
-        cost_estimate=pl.CostEstimate(
-            flops=8 * poles * elems, bytes_accessed=8 * elems, transcendentals=0
-        ),
         name="conv",
-    )(lengths, mixed, q_feat, pole_rate, residue, skip_gain[None, :], incoming, got)
+    )(
+        lengths, end, span, base, coef, pole_rate, residue, skip_gain[None, :], mixed, q_feat
+    )
     return mixed_out, decode_state
 
 

time: 50.4 us -> 40.7 us (0.81)
  the two profiles are of different devices: /device:TPU:0 before, /device:TPU:16 now
where the time goes in v4:
time: 40.7 us; the launch traced here: 40.4 us
  Pallas kernels  35.9 us (88%)
  local copies, waits for them, and re-layouts  3.85 us (9%)
  between operations  0.65 us (2%)
    pallas_call x1, Pallas kernels, shards(): pl.pallas_call(functools.partial(conv_kernel, hops=hops, parts=parts, til...  25.8 us
    pallas_call x1, Pallas kernels, shards(): pl.pallas_call(functools.partial(ends_kernel, **sizes), grid_spec=pltpu.P...  10.2 us
    unnamed x4, local copies, waits for them, and re-layouts  3.85 us

profile of v4, /device:TPU:16, one launch (start us, length us, event | category | flops | bytes accessed | tf_op | source)
XLA Modules:
  0.0 40.4 jit_solution(13236783521635230031)
XLA Ops:
  0.6 10.2 %ends.1 = (f32[8192,128]{1,0:T(8,128)}, f32[16,2048]{1,0:T(8,128)}, f32[16,2048]{1,0:T(8,128)}, f32[4,16,2048]{2,1,0:T(8,128)}, f32[4,16,2048]{2,1,0:T(8,128)}) custom-call(s32[4]{0:T(128)} %lens_ref.3, s32[4]{0:T(128)} %own_ref.1, bf16[512,2048]{1,0:T(8,128)(2,1)} %k_ref.1, bf16[512,2048]{1,0:T(8,128)(2,1)} %v_ref.1, f32[16,2048]{1,0:T(8,128)} %rate_ref.3), custom_call_target="tpu_custom_call" | custom-call | flops 33554432 | bytes 8388608 | tf_op jit(solution)/shard_map/ends/pallas_call | solution.py:315
  10.8 25.8 %conv.1 = (bf16[512,2048]{1,0:T(8,128)(2,1)}, f32[1,16,2048]{2,1,0:T(8,128)}) custom-call(s32[4]{0:T(128)} %lens_ref.3, f32[16,2048]{1,0:T(8,128)} %get-tuple-element.7.end_ref, f32[16,2048]{1,0:T(8,128)} %get-tuple-element.8.span_ref, f32[4,16,2048]{2,1,0:T(8,128)} %get-tuple-element.9.base_ref, f32[4,16,2048]{2,1,0:T(8,128)} %get-tuple-element.10.coef_ref, ...), custom_call_target="tpu_custom_call" | custom-call | tf_op jit(solution)/shard_map/conv/pallas_call | solution.py:342
  36.6 0.0 copy-start
  36.6 3.2 %copy.12 = bf16[512,2048]{1,0:T(8,128)(2,1)} copy(bf16[512,2048]{1,0:T(8,128)(2,1)} %get-tuple-element.14) | data formatting | bytes 4194304
  39.8 0.0 copy-done
  39.8 0.7 %copy.13 = f32[1,16,2048]{2,1,0:T(8,128)} copy(f32[1,16,2048]{2,1,0:T(8,128)S(1)} %copy-done) | data formatting | bytes 262144
Async XLA Ops:
  36.6 3.2 %copy-start = (f32[1,16,2048]{2,1,0:T(8,128)S(1)}, f32[1,16,2048]{2,1,0:T(8,128)}, u32[]{:S(2)}) copy-start(f32[1,16,2048]{2,1,0:T(8,128)} %get-tuple-element.15) | copy-start | bytes 393220

commit v5 on v4

--- a/solution.py
+++ b/solution.py
@@ -106,11 +106,11 @@
 
 
 def conv_kernel(
-    lens_ref, end_ref, span_ref, base_ref, coef_ref, rate_ref, res_ref, gain_ref, u_hbm, q_hbm,
-    out_hbm, got_ref,
+    lens_ref, end_ref, span_ref, base_ref, coef_ref, rate_ref, res_ref, gain_ref, u_hbm,
+    conv_hbm, got_ref,
     arrived, passed, slotted, landed, decay_sc, res_sc, state_sc, gain_sc, conv_sc,
-    u_ref, q_ref, out_ref, sent_sem, come_sem, give_sem, take_sem, load_sem, store_sem,
-    *, hops, parts, tok, sub, poles, count, chunk, tiles,
+    u_ref, sent_sem, come_sem, give_sem, take_sem, load_sem, store_sem,
+    *, hops, parts, tok, sub, poles, count, tiles,
 ):
     slots, _, channels = base_ref.shape
     width = channels // parts
@@ -125,15 +125,11 @@
         )
     loads = []
     for i in range(tiles):
-        flat, cols = pl.ds(i * rows_in, rows_in), pl.ds(i * wide, wide)
+        flat = pl.ds(i * rows_in, rows_in)
         loads.append(
-            (
-                pltpu.make_async_copy(u_hbm.at[flat, :], u_ref.at[flat, :], load_sem.at[i, 0]),
-                pltpu.make_async_copy(q_hbm.at[:, cols], q_ref.at[:, cols], load_sem.at[i, 1]),
-            )
+            pltpu.make_async_copy(u_hbm.at[flat, :], u_ref.at[flat, :], load_sem.at[i])
         )
-        loads[i][0].start()
-        loads[i][1].start()
+        loads[i].start()
     pl.semaphore_wait(barrier, slots - 1)
 
     def lanes(part):
@@ -212,8 +208,8 @@
                 for at in starts:
                     keep = keep - (t == at).astype(jnp.int32)
                 pick = jnp.maximum(keep, 0) * poles
-                rows = pl.ds(pl.multiple_of(t * sub, sub), sub)
-                u = u_ref[pl.ds(pl.multiple_of(i * rows_in + t * sub, sub), sub), :]
+                rows = pl.ds(pl.multiple_of(i * rows_in + t * sub, sub), sub)
+                u = u_ref[rows, :]
                 state = tuple(decay_sc[pick + p] * s + u for p, s in enumerate(state))
                 terms = [gain * u] + [c * s for c, s in zip(scale, state)]
                 while len(terms) > 1:
@@ -227,6 +223,13 @@
         state = lax.fori_loop(begin // UNROLL, stop // UNROLL, many, state)
         for p in range(poles):
             state_sc[p] = state[p]
+        rows = pl.ds(i * rows_in + begin * sub, (stop - begin) * sub)
+        stores.append(
+            pltpu.make_async_copy(
+                conv_sc.at[rows, :], conv_hbm.at[rows, :], store_sem.at[len(stores)]
+            )
+        )
+        stores[-1].start()
 
     def scatter(value, ref, base):
         for p in range(poles):
@@ -248,33 +251,13 @@
             for part in range(per_tile):
                 finish(part)
         scatter(arrived[hops - 1, :, cols], state_sc, 0)
-        loads[i][0].wait()
-        if i == 0 and tiles > 1:
-            conv(i, 0, tok // 4)
+        loads[i].wait()
+        cut = tok // 4 if i == 0 else tok - tok // 4
+        conv(i, 0, cut)
+        if i == 0:
             for part in range(per_tile, parts):
                 finish(part)
-            conv(i, tok // 4, tok)
-        else:
-            conv(i, 0, tok)
-        loads[i][1].wait()
-
-        def gate(n, _):
-            start = pl.multiple_of(n * chunk, chunk)
-            rows = pl.ds(start, chunk)
-            for j in range(sub):
-                at = slice(i * wide + j * LANES, i * wide + (j + 1) * LANES)
-                value = conv_sc[pl.ds(start * sub + j, chunk, stride=sub), :]
-                out_ref[rows, at] = (q_ref[rows, at].astype(F32) * value).astype(out_ref.dtype)
-            return 0
-
-        lax.fori_loop(0, tok // chunk, gate, 0)
-        stores.append(
-            pltpu.make_async_copy(
-                out_ref.at[:, pl.ds(i * wide, wide)], out_hbm.at[:, pl.ds(i * wide, wide)],
-                store_sem.at[i],
-            )
-        )
-        stores[i].start()
+        conv(i, cut, tok)
 
     for part in range(parts):
         at = lanes(part)
@@ -298,6 +281,21 @@
         copy.wait()
 
 
+def gate_kernel(conv_ref, q_ref, got_ref, out_ref, kept_ref, *, sub, chunk):
+    kept_ref[...] = got_ref[...]
+
+    def gate(n, _):
+        start = pl.multiple_of(n * chunk, chunk)
+        rows = pl.ds(start, chunk)
+        for j in range(sub):
+            at = slice(j * LANES, (j + 1) * LANES)
+            value = conv_ref[pl.ds(start * sub + j, chunk, stride=sub), :]
+            out_ref[rows, at] = (q_ref[rows, at].astype(F32) * value).astype(out_ref.dtype)
+        return 0
+
+    lax.fori_loop(0, q_ref.shape[0] // chunk, gate, 0)
+
+
 def shards(q_feat, k_feat, v_feat, pole_rate, residue, skip_gain, lengths, owners):
     tok, channels = q_feat.shape
     poles, count = pole_rate.shape[0], lengths.shape[0]
@@ -305,7 +303,8 @@
     sub = min(ROWS, channels // LANES)
     width = sub * LANES
     tiles = channels // width
-    sizes = dict(tok=tok, sub=sub, poles=poles, count=count, chunk=16)
+    shape = dict(tok=tok, sub=sub, poles=poles, count=count)
+    sizes = dict(shape, chunk=16)
     feat = pl.BlockSpec((tok, width), lambda i, *_: (0, i))
     pole = pl.BlockSpec((poles, width), lambda i, *_: (0, i))
     slot = pl.BlockSpec((slots, poles, width), lambda i, *_: (0, 0, i))
@@ -339,12 +338,12 @@
     parts = max(tiles, min(4, channels // LANES))
     dma = pltpu.SemaphoreType.DMA
     vmem, hbm = pl.BlockSpec(memory_space=pltpu.VMEM), pl.BlockSpec(memory_space=pl.ANY)
-    mixed_out, decode_state = pl.pallas_call(
-        functools.partial(conv_kernel, hops=hops, parts=parts, tiles=tiles, **sizes),
-        in_specs=[pl.BlockSpec(memory_space=pltpu.SMEM)] + [vmem] * 7 + [hbm] * 2,
+    conv, got = pl.pallas_call(
+        functools.partial(conv_kernel, hops=hops, parts=parts, tiles=tiles, **shape),
+        in_specs=[pl.BlockSpec(memory_space=pltpu.SMEM)] + [vmem] * 7 + [hbm],
         out_specs=[hbm, vmem],
         out_shape=[
-            jax.ShapeDtypeStruct((tok, channels), q_feat.dtype),
+            jax.ShapeDtypeStruct((tiles * tok * sub, LANES), F32),
             jax.ShapeDtypeStruct((1, poles, channels), F32),
         ],
         scratch_shapes=[
@@ -356,19 +355,34 @@
             pltpu.VMEM((poles, sub, LANES), F32),
             pltpu.VMEM((poles, sub, LANES), F32),
             pltpu.VMEM((sub, LANES), F32),
-            pltpu.VMEM((tok * sub, LANES), F32),
             pltpu.VMEM((tiles * tok * sub, LANES), F32),
-            pltpu.VMEM((tok, channels), q_feat.dtype),
-            pltpu.VMEM((tok, channels), q_feat.dtype),
+            pltpu.VMEM((tiles * tok * sub, LANES), F32),
             dma((hops, parts)), dma((hops, parts)),
             dma((slots - 1, parts)), dma((slots - 1, parts)),
-            dma((tiles, 2)), dma((tiles,)),
+            dma((tiles,)), dma((2 * tiles,)),
         ],
         compiler_params=pltpu.CompilerParams(collective_id=0, has_side_effects=True),
         name="conv",
     )(
-        lengths, end, span, base, coef, pole_rate, residue, skip_gain[None, :], mixed, q_feat
+        lengths, end, span, base, coef, pole_rate, residue, skip_gain[None, :], mixed
     )
+    cuts = 4
+    rows = tok // cuts
+    block = pl.BlockSpec((rows, width), lambda i, n: (n, i))
+    whole = pl.BlockSpec((1, poles, channels), lambda i, n: (0, 0, 0))
+    mixed_out, decode_state = pl.pallas_call(
+        functools.partial(gate_kernel, sub=sub, chunk=16),
+        grid=(tiles, cuts),
+        in_specs=[
+            pl.BlockSpec((rows * sub, LANES), lambda i, n: (i * cuts + n, 0)), block, whole
+        ],
+        out_specs=[block, whole],
+        out_shape=[
+            jax.ShapeDtypeStruct((tok, channels), q_feat.dtype),
+            jax.ShapeDtypeStruct((1, poles, channels), F32),
+        ],
+        name="gate",
+    )(conv, q_feat, got)
     return mixed_out, decode_state
 
 

time: 40.7 us -> 43 us (1.057)
  the two profiles are of different devices: /device:TPU:16 before, /device:TPU:0 now
where the time goes in v5:
time: 43 us; the launch traced here: 42.7 us
  Pallas kernels  42.1 us (98%)
  between operations  0.64 us (1%)
    pallas_call x1, Pallas kernels, shards(): pl.pallas_call(functools.partial(conv_kernel, hops=hops, parts=parts, til...  25.1 us
    pallas_call x1, Pallas kernels, shards(): pl.pallas_call(functools.partial(ends_kernel, **sizes), grid_spec=pltpu.P...  10 us
    pallas_call x1, Pallas kernels, shards(): pl.pallas_call(functools.partial(gate_kernel, sub=sub, chunk=16), grid=(t...  6.98 us

profile of v5, /device:TPU:0, one launch (start us, length us, event | category | flops | bytes accessed | tf_op | source)
XLA Modules:
  0.0 42.7 jit_solution(17097730544109572293)
XLA Ops:
  0.6 10.0 %ends.1 = (f32[8192,128]{1,0:T(8,128)}, f32[16,2048]{1,0:T(8,128)}, f32[16,2048]{1,0:T(8,128)}, f32[4,16,2048]{2,1,0:T(8,128)}, f32[4,16,2048]{2,1,0:T(8,128)}) custom-call(s32[4]{0:T(128)} %lens_ref.3, s32[4]{0:T(128)} %own_ref.1, bf16[512,2048]{1,0:T(8,128)(2,1)} %k_ref.1, bf16[512,2048]{1,0:T(8,128)(2,1)} %v_ref.1, f32[16,2048]{1,0:T(8,128)} %rate_ref.3), custom_call_target="tpu_custom_call" | custom-call | flops 33554432 | bytes 8388608 | tf_op jit(solution)/shard_map/ends/pallas_call | solution.py:314
  10.7 25.1 %conv.1 = (f32[8192,128]{1,0:T(8,128)}, f32[1,16,2048]{2,1,0:T(8,128)}) custom-call(s32[4]{0:T(128)} %lens_ref.3, f32[16,2048]{1,0:T(8,128)} %get-tuple-element.9.end_ref, f32[16,2048]{1,0:T(8,128)} %get-tuple-element.10.span_ref, f32[4,16,2048]{2,1,0:T(8,128)} %get-tuple-element.11.base_ref, f32[4,16,2048]{2,1,0:T(8,128)} %get-tuple-element.12.coef_ref, ...), custom_call_target="tpu_custom_call" | custom-call | tf_op jit(solution)/shard_map/conv/pallas_call | solution.py:341
  35.8 7.0 %gate.1 = (bf16[512,2048]{1,0:T(8,128)(2,1)}, f32[1,16,2048]{2,1,0:T(8,128)}) custom-call(f32[8192,128]{1,0:T(8,128)} %get-tuple-element.14.conv_ref, bf16[512,2048]{1,0:T(8,128)(2,1)} %q_ref.1, f32[1,16,2048]{2,1,0:T(8,128)} %get-tuple-element.15.got_ref), custom_call_target="tpu_custom_call" | custom-call | tf_op jit(solution)/shard_map/gate/pallas_call | solution.py:373

commit v6 on v4

--- a/solution.py
+++ b/solution.py
@@ -234,7 +234,6 @@
                 ref[base + p, j : j + 1, :] = value[p : p + 1, j * LANES : (j + 1) * LANES]
 
     stores = []
-    per_tile = parts // tiles
     for i in range(tiles):
         cols = slice(i * wide, (i + 1) * wide)
         rate = rate_ref[:, cols]
@@ -245,17 +244,11 @@
             at = i * wide + j * LANES
             gain_sc[j : j + 1, :] = gain_ref[0:1, at : at + LANES]
         if i == 0:
-            for part in range(per_tile):
+            for part in range(parts):
                 finish(part)
         scatter(arrived[hops - 1, :, cols], state_sc, 0)
         loads[i][0].wait()
-        if i == 0 and tiles > 1:
-            conv(i, 0, tok // 4)
-            for part in range(per_tile, parts):
-                finish(part)
-            conv(i, tok // 4, tok)
-        else:
-            conv(i, 0, tok)
+        conv(i, 0, tok)
         loads[i][1].wait()
 
         def gate(n, _):

time: 40.7 us -> 42.2 us (1.037)
  Pallas kernels: 35.9 us -> 37.4 us
    pallas_call x1, Pallas kernels: 25.8 us -> 27.3 us  [shards(): pl.pallas_call(functools.partial(conv_kernel, hops=hops, parts=parts, til...]
where the time goes in v6:
time: 42.2 us; the launch traced here: 41.9 us
  Pallas kernels  37.4 us (89%)
  local copies, waits for them, and re-layouts  3.85 us (9%)
  between operations  0.65 us (2%)
    pallas_call x1, Pallas kernels, shards(): pl.pallas_call(functools.partial(conv_kernel, hops=hops, parts=parts, til...  27.3 us
    pallas_call x1, Pallas kernels, shards(): pl.pallas_call(functools.partial(ends_kernel, **sizes), grid_spec=pltpu.P...  10.1 us
    unnamed x4, local copies, waits for them, and re-layouts  3.85 us

profile of v6, /device:TPU:16, one launch (start us, length us, event | category | flops | bytes accessed | tf_op | source)
XLA Modules:
  0.0 41.9 jit_solution(15588530433416187756)
XLA Ops:
  0.6 10.1 %ends.1 = (f32[8192,128]{1,0:T(8,128)}, f32[16,2048]{1,0:T(8,128)}, f32[16,2048]{1,0:T(8,128)}, f32[4,16,2048]{2,1,0:T(8,128)}, f32[4,16,2048]{2,1,0:T(8,128)}) custom-call(s32[4]{0:T(128)} %lens_ref.3, s32[4]{0:T(128)} %own_ref.1, bf16[512,2048]{1,0:T(8,128)(2,1)} %k_ref.1, bf16[512,2048]{1,0:T(8,128)(2,1)} %v_ref.1, f32[16,2048]{1,0:T(8,128)} %rate_ref.3), custom_call_target="tpu_custom_call" | custom-call | flops 33554432 | bytes 8388608 | tf_op jit(solution)/shard_map/ends/pallas_call | solution.py:308
  10.7 27.3 %conv.1 = (bf16[512,2048]{1,0:T(8,128)(2,1)}, f32[1,16,2048]{2,1,0:T(8,128)}) custom-call(s32[4]{0:T(128)} %lens_ref.3, f32[16,2048]{1,0:T(8,128)} %get-tuple-element.7.end_ref, f32[16,2048]{1,0:T(8,128)} %get-tuple-element.8.span_ref, f32[4,16,2048]{2,1,0:T(8,128)} %get-tuple-element.9.base_ref, f32[4,16,2048]{2,1,0:T(8,128)} %get-tuple-element.10.coef_ref, ...), custom_call_target="tpu_custom_call" | custom-call | tf_op jit(solution)/shard_map/conv/pallas_call | solution.py:335
  38.1 0.0 copy-start
  38.1 3.2 %copy.12 = bf16[512,2048]{1,0:T(8,128)(2,1)} copy(bf16[512,2048]{1,0:T(8,128)(2,1)} %get-tuple-element.14) | data formatting | bytes 4194304
  41.3 0.0 copy-done
  41.3 0.7 %copy.13 = f32[1,16,2048]{2,1,0:T(8,128)} copy(f32[1,16,2048]{2,1,0:T(8,128)S(1)} %copy-done) | data formatting | bytes 262144
Async XLA Ops:
  38.1 3.2 %copy-start = (f32[1,16,2048]{2,1,0:T(8,128)S(1)}, f32[1,16,2048]{2,1,0:T(8,128)}, u32[]{:S(2)}) copy-start(f32[1,16,2048]{2,1,0:T(8,128)} %get-tuple-element.15) | copy-start | bytes 393220

commit v7 on v4

--- a/solution.py
+++ b/solution.py
@@ -11,6 +11,7 @@
 LANES = 128
 ROWS = 8
 UNROLL = 8
+DEEP = 16
 
 
 def spans(lens_ref, count, tok):
@@ -206,8 +207,8 @@
         gain = gain_sc[...]
 
         def many(n, state):
-            for k in range(UNROLL):
-                t = n * UNROLL + k
+            for k in range(DEEP):
+                t = n * DEEP + k
                 keep = jnp.int32(1)
                 for at in starts:
                     keep = keep - (t == at).astype(jnp.int32)
@@ -224,7 +225,7 @@
             return state
 
         state = tuple(state_sc[p] for p in range(poles))
-        state = lax.fori_loop(begin // UNROLL, stop // UNROLL, many, state)
+        state = lax.fori_loop(begin // DEEP, stop // DEEP, many, state)
         for p in range(poles):
             state_sc[p] = state[p]
 

time: 40.7 us -> 39.9 us (0.980)
  the two profiles are of different devices: /device:TPU:16 before, /device:TPU:0 now
where the time goes in v7:
time: 39.9 us; the launch traced here: 39.7 us
  Pallas kernels  35.2 us (88%)
  local copies, waits for them, and re-layouts  3.85 us (10%)
  between operations  0.65 us (2%)
    pallas_call x1, Pallas kernels, shards(): pl.pallas_call(functools.partial(conv_kernel, hops=hops, parts=parts, til...  25.3 us
    pallas_call x1, Pallas kernels, shards(): pl.pallas_call(functools.partial(ends_kernel, **sizes), grid_spec=pltpu.P...  9.94 us
    unnamed x4, local copies, waits for them, and re-layouts  3.85 us

profile of v7, /device:TPU:0, one launch (start us, length us, event | category | flops | bytes accessed | tf_op | source)
XLA Modules:
  0.0 39.7 jit_solution(16844573038139662240)
XLA Ops:
  0.6 9.9 %ends.1 = (f32[8192,128]{1,0:T(8,128)}, f32[16,2048]{1,0:T(8,128)}, f32[16,2048]{1,0:T(8,128)}, f32[4,16,2048]{2,1,0:T(8,128)}, f32[4,16,2048]{2,1,0:T(8,128)}) custom-call(s32[4]{0:T(128)} %lens_ref.3, s32[4]{0:T(128)} %own_ref.1, bf16[512,2048]{1,0:T(8,128)(2,1)} %k_ref.1, bf16[512,2048]{1,0:T(8,128)(2,1)} %v_ref.1, f32[16,2048]{1,0:T(8,128)} %rate_ref.3), custom_call_target="tpu_custom_call" | custom-call | flops 33554432 | bytes 8388608 | tf_op jit(solution)/shard_map/ends/pallas_call | solution.py:316
  10.6 25.3 %conv.1 = (bf16[512,2048]{1,0:T(8,128)(2,1)}, f32[1,16,2048]{2,1,0:T(8,128)}) custom-call(s32[4]{0:T(128)} %lens_ref.3, f32[16,2048]{1,0:T(8,128)} %get-tuple-element.7.end_ref, f32[16,2048]{1,0:T(8,128)} %get-tuple-element.8.span_ref, f32[4,16,2048]{2,1,0:T(8,128)} %get-tuple-element.9.base_ref, f32[4,16,2048]{2,1,0:T(8,128)} %get-tuple-element.10.coef_ref, ...), custom_call_target="tpu_custom_call" | custom-call | tf_op jit(solution)/shard_map/conv/pallas_call | solution.py:343
  35.8 0.0 copy-start
  35.9 3.2 %copy.12 = bf16[512,2048]{1,0:T(8,128)(2,1)} copy(bf16[512,2048]{1,0:T(8,128)(2,1)} %get-tuple-element.14) | data formatting | bytes 4194304
  39.0 0.0 copy-done
  39.0 0.7 %copy.13 = f32[1,16,2048]{2,1,0:T(8,128)} copy(f32[1,16,2048]{2,1,0:T(8,128)S(1)} %copy-done) | data formatting | bytes 262144
Async XLA Ops:
  35.8 3.2 %copy-start = (f32[1,16,2048]{2,1,0:T(8,128)S(1)}, f32[1,16,2048]{2,1,0:T(8,128)}, u32[]{:S(2)}) copy-start(f32[1,16,2048]{2,1,0:T(8,128)} %get-tuple-element.15) | copy-start | bytes 393220
